TPU v7x, 128 devices: a whole 4x4x4 slice. The times are simulated.
128 devices in a mesh: gx: 8 (over y, core), gy: 16 (over z, x).
Axes of the slice: x: 4, y: 4, z: 4, core: 2. Of those that a mesh axis runs over, the one named last changes fastest.
Arguments:
- model_state: float32 [3, 8, 3072, 2048], P(None, None, 'gx', 'gy'), may hold values from -6 to 6
- obs_val: float32 [16384, 384], P(('gx', 'gy')), may hold values from -6 to 6
- obs_owner: int32 [16384, 1], P(('gx', 'gy')), may hold values from 0 to 15; in each aligned block of 128 rows (0 to 127, 128 to 255, ...) at most 16 rows name the same one
- obs_x: int32 [16384], P(('gx', 'gy')), may hold values from 0 to 3071
- obs_y: int32 [16384], P(('gx', 'gy')), may hold values from 0 to 127
- cressman: float32 [3072, 3072], P(None, 'gx'), as said below
- vertical: float32 [3, 8, 128], replicated, may hold values from -2 to 2
Outputs:
- new_state: float32 [3, 8, 3072, 2048], P(None, None, 'gx', 'gy')
Inputs may be any that keep to these rules, and one draw needn't show every extreme that they name: `obs_owner`: among the rows of one device, at most 16 name one column; in every draw some device's rows name some column exactly 16 times. `cressman`: entries are positive.
All inputs are finite; a program needn't handle non-finite values.
Results may differ from a plain program's by a relative error of at most 0.0001.
Values sent between devices are 32-bit elements; how exact they have to be, the bound alone decides.
A program may use at most 128 MiB of HBM per device.

v0:
```python
import math

import jax
import jax.numpy as jnp
from jax import lax
from jax.sharding import PartitionSpec as P

advect_coef = 0.5
diffuse_h = 0.2
diffuse_z = 0.1
time_step = 0.5
nudge_gain = 1.0
spread_gain = 0.125


def with_halo(value, sides, width):
    for axis, dim in sides:
        devices, length = (lax.axis_size(axis), value.shape[dim])
        up = [(i, (i + 1) % devices) for i in range(devices - 1)]
        down = [(j, i) for i, j in up]
        last = lax.slice_in_dim(value, length - width, length, axis=dim)
        initial = lax.slice_in_dim(value, 0, width, axis=dim)
        before = lax.ppermute(last, axis, up)
        after = lax.ppermute(initial, axis, down)
        value = jnp.concatenate([before, value, after], axis=dim)
    return value


def tendency(padded):
    center = padded[:, :, 1:-1, 1:-1]
    to_east = padded[:, :, 2:, 1:-1]
    to_west = padded[:, :, :-2, 1:-1]
    to_north = padded[:, :, 1:-1, 2:]
    to_south = padded[:, :, 1:-1, :-2]
    wind_u = center[0][None]
    wind_v = center[1][None]
    advection = -0.5 * advect_coef * (wind_u * (to_east - to_west) + wind_v * (to_north - to_south))
    laplace = to_east + to_west + to_north + to_south - 4.0 * center
    upper_cells = jnp.concatenate([center[:, 1:], center[:, -1:]], axis=1)
    lower_cells = jnp.concatenate([center[:, :1], center[:, :-1]], axis=1)
    return advection + diffuse_h * laplace + diffuse_z * (upper_cells + lower_cells - 2.0 * center)


def column_sums(model_state, record_meta, cressman):
    fields, levels, tile_x, tile_y = model_state.shape
    slots = record_meta.shape[0]
    block = math.gcd(slots, 512)
    blocks = slots // block
    flattened = model_state.reshape(fields * levels * tile_x, tile_y)

    def column_per_block(piece):
        x_cells, y_cells = piece
        weight = jnp.take(cressman, x_cells, axis=0)
        picker = (y_cells[:, None] == jnp.arange(tile_y, dtype=jnp.int32)[None, :]).astype(
            jnp.float32
        )
        picked = lax.dot_general(
            flattened, picker, (((1,), (1,)), ((), ())), precision=lax.Precision.HIGHEST
        )
        picked = picked.reshape(fields * levels, tile_x, block)
        colsum = jnp.einsum("kxb,bx->bk", picked, weight, precision=lax.Precision.HIGHEST)
        return (colsum, jnp.sum(weight, axis=1))

    pieces = (record_meta[:, 0].reshape(blocks, block), record_meta[:, 1].reshape(blocks, block))
    colsum, row_parts = lax.map(column_per_block, pieces)
    return (colsum.reshape(slots, fields * levels), row_parts.reshape(slots))


def innovations(colsum, totals, values, validity, vertical):
    fields, levels, obs_levels = vertical.shape
    averaged = (colsum / totals[:, None]).reshape(-1, fields, levels)
    model_eq = jnp.einsum("svz,vzl->svl", averaged, vertical, precision=lax.Precision.HIGHEST)
    innovation = (values.reshape(-1, fields, obs_levels) - model_eq) * validity[:, None, None]
    spread = (
        jnp.einsum("svl,vzl->svz", innovation, vertical, precision=lax.Precision.HIGHEST)
        * spread_gain
    )
    return spread.reshape(-1, fields * levels)


def spread_back(spread, record_meta, cressman, tile_shape):
    fields, levels, tile_x, tile_y = tile_shape
    slots = record_meta.shape[0]
    block = math.gcd(slots, 512)
    blocks = slots // block

    def spread_per_block(running, piece):
        numer, weights_sum = running
        x_cells, y_cells, validity, increments = piece
        weight = jnp.take(cressman, x_cells, axis=0) * validity[:, None]
        picker = (y_cells[:, None] == jnp.arange(tile_y, dtype=jnp.int32)[None, :]).astype(
            jnp.float32
        )
        weighted = (increments[:, :, None] * weight[:, None, :]).reshape(
            block, fields * levels * tile_x
        )
        numer = numer + lax.dot_general(
            weighted, picker, (((0,), (0,)), ((), ())), precision=lax.Precision.HIGHEST
        )
        weights_sum = weights_sum + lax.dot_general(
            weight, picker, (((0,), (0,)), ((), ())), precision=lax.Precision.HIGHEST
        )
        return ((numer, weights_sum), None)

    start = (
        jnp.zeros((fields * levels * tile_x, tile_y), jnp.float32),
        jnp.zeros((tile_x, tile_y), jnp.float32),
    )
    pieces = (
        record_meta[:, 0].reshape(blocks, block),
        record_meta[:, 1].reshape(blocks, block),
        record_meta[:, 2].astype(jnp.float32).reshape(blocks, block),
        spread.reshape(blocks, block, fields * levels),
    )
    (numer, weights_sum), _ = lax.scan(spread_per_block, start, pieces)
    return (numer.reshape(tile_shape), weights_sum)


def local(model_state, obs_val, obs_owner, obs_x, obs_y, cressman, vertical):
    count_x = lax.axis_size("gx")
    count_y = lax.axis_size("gy")
    records = obs_val.shape[0]
    capacity = max(2, 2 * records // count_y)
    padded = with_halo(model_state, (("gx", 2), ("gy", 3)), 1)
    column = obs_owner[:, 0]
    onehot = (column[:, None] == jnp.arange(count_y, dtype=jnp.int32)[None, :]).astype(jnp.int32)
    before = jnp.cumsum(onehot, axis=0) - onehot
    rank_in = jnp.sum(before * onehot, axis=1)
    slot_index = column * capacity + rank_in
    record_meta = jnp.stack([obs_x, obs_y, jnp.ones_like(obs_x)], axis=1)
    send_values = (
        jnp.zeros((count_y * capacity, obs_val.shape[1]), jnp.float32).at[slot_index].set(obs_val)
    )
    send_meta = jnp.zeros((count_y * capacity, 3), jnp.int32).at[slot_index].set(record_meta)
    col_values, col_meta = (
        lax.all_to_all(
            jnp.tile(send_values, (count_x, 1)),
            ("gx", "gy"),
            split_axis=0,
            concat_axis=0,
            tiled=True,
        ),
        lax.all_to_all(
            jnp.tile(send_meta, (count_x, 1)), ("gx", "gy"), split_axis=0, concat_axis=0, tiled=True
        ),
    )
    colsum, row_parts = column_sums(model_state, col_meta, cressman)
    summed, totals = lax.psum((colsum, row_parts), "gx")
    spread = innovations(summed, totals, col_values, col_meta[:, 2].astype(jnp.float32), vertical)
    numer, weights_sum = spread_back(spread, col_meta, cressman, model_state.shape)
    nudge = numer / jnp.maximum(weights_sum, 1.0)[None, None]
    return model_state + time_step * (tendency(padded) + nudge_gain * nudge)


def solution(mesh):
    in_specs = (
        P(None, None, "gx", "gy"),
        P(("gx", "gy"), None),
        P(("gx", "gy"), None),
        P(("gx", "gy")),
        P(("gx", "gy")),
        P(None, "gx"),
        P(),
    )
    out_specs = P(None, None, "gx", "gy")
    return jax.shard_map(local, mesh=mesh, in_specs=in_specs, out_specs=out_specs, check_vma=False)
```

profile of v0, /device:TPU:5, one launch (start us, length us, event | category | flops | bytes accessed | tf_op | source)
XLA Modules:
  0.0 514.8 jit_solution(14981629406584636861)
XLA Ops:
  11.9 10.8 %all-to-all-start.1 = ((s32[128,16,3]{1,2,0:T(4,128)}), s32[128,16,3]{1,2,0:T(4,128)S(1)}, u32[]{:S(2)}, u32[]{:S(2)}) async-start(s32[128,16,3]{1,2,0:T(4,128)} %copy.46), calls=%async_computation.1 | async-start | bytes 524288 | tf_op jit(solution)/shard_map/all_to_all | solution.py:143
  26.0 3.6 collective-permute-start.1
  29.5 7.6 %fusion.37 = (f32[3,7,384,128]{3,2,1,0:T(8,128)}, f32[3,7,384,128]{3,2,1,0:T(8,128)}) fusion(f32[3,8,384,128]{3,2,1,0:T(8,128)} %param.13), kind=kLoop, calls=%fused_computation.78 | loop fusion | bytes 16515072 | tf_op jit(solution)/shard_map/slice | solution.py:40
  41.7 2.7 pad_maximum_fusion
  44.4 5.2 %fusion.34 = (f32[3,8,386,1]{3,2,1,0:T(8,128)}, f32[3,8,386,1]{3,2,1,0:T(8,128)}) fusion(f32[3,8,386,128]{3,2,1,0:T(8,128)S(1)} %pad_maximum_fusion), kind=kLoop, calls=%fused_computation.75 | loop fusion | bytes 148224 | tf_op jit(solution)/shard_map/slice | solution.py:21
  49.7 4.1 copy.40
  56.0 4.1 copy.42
  60.0 3.1 collective-permute-start.3
  65.0 11.7 %all-to-all-start = ((f32[128,16,384]{2,1,0:T(8,128)}), f32[128,16,384]{2,1,0:T(8,128)}, u32[]{:S(2)}, u32[]{:S(2)}) async-start(f32[128,16,384]{2,1,0:T(8,128)} %bitcast.12), calls=%async_computation | async-start | bytes 6291456 | tf_op jit(solution)/shard_map/all_to_all | solution.py:136
  77.0 176.2 %while.25 = (s32[]{:T(128)}, f32[4,512,24]{1,0,2:T(4,128)S(1)}, f32[4,512]{1,0:T(4,128)S(1)}, s32[4,512]{1,0:T(4,128)S(1)}, f32[9216,128]{1,0:T(8,128)}, /*index...) while((s32[]{:T(128)}, f32[4,512,24]{1,0,2:T(4,128)S(1)}, f32[4,512]{1,0:T(4,128)S(1)}, ...), condition=%wide.region_6.8_spmd, body=%wide.region_4.7_spmd.sunk | while | flops 7304844288 | bytes 84524128 | solution.py:65
  77.6 4.2 gather_fusion
  82.0 9.7 %fusion.54 = f32[512,9216]{1,0:T(8,128)S(1)} fusion(f32[9216,128]{1,0:T(8,128)} %get-tuple-element.325, s32[512]{0:T(512)S(1)} %bitcast.112), kind=kOutput, calls=%fused_computation.9.clone.1 | convolution fusion | flops 7247822848 | bytes 23595008 | tf_op jit(solution)/shard_map/while/body/eval_jaxpr/dot_general | solution.py:57
  91.7 4.8 copy.78
  96.6 23.4 %fusion.55 = f32[512,1,24]{2,1,0:T(1,128)S(1)} fusion(f32[24,384,512]{1,0,2:T(8,128)S(1)} %bitcast.102, f32[512,384,1]{1,0,2:T(8,128)S(1)} %get-tuple-element.291), kind=kOutput, calls=%fused_computation.4.clone.1 | convolution fusion | flops 56623104 | bytes 19709952 | tf_op jit(solution)/shard_map/while/body/eval_jaxpr/kxb,bx->bk/dot_general | solution.py:61
  121.5 4.2 gather_fusion
  125.9 9.7 %fusion.54 = f32[512,9216]{1,0:T(8,128)S(1)} fusion(f32[9216,128]{1,0:T(8,128)} %get-tuple-element.325, s32[512]{0:T(512)S(1)} %bitcast.112), kind=kOutput, calls=%fused_computation.9.clone.1 | convolution fusion | flops 7247822848 | bytes 23595008 | tf_op jit(solution)/shard_map/while/body/eval_jaxpr/dot_general | solution.py:57
  135.6 4.8 copy.78
  140.5 23.4 %fusion.55 = f32[512,1,24]{2,1,0:T(1,128)S(1)} fusion(f32[24,384,512]{1,0,2:T(8,128)S(1)} %bitcast.102, f32[512,384,1]{1,0,2:T(8,128)S(1)} %get-tuple-element.291), kind=kOutput, calls=%fused_computation.4.clone.1 | convolution fusion | flops 56623104 | bytes 19709952 | tf_op jit(solution)/shard_map/while/body/eval_jaxpr/kxb,bx->bk/dot_general | solution.py:61
  165.4 4.2 gather_fusion
  169.8 9.7 %fusion.54 = f32[512,9216]{1,0:T(8,128)S(1)} fusion(f32[9216,128]{1,0:T(8,128)} %get-tuple-element.325, s32[512]{0:T(512)S(1)} %bitcast.112), kind=kOutput, calls=%fused_computation.9.clone.1 | convolution fusion | flops 7247822848 | bytes 23595008 | tf_op jit(solution)/shard_map/while/body/eval_jaxpr/dot_general | solution.py:57
  179.5 4.8 copy.78
  184.4 23.4 %fusion.55 = f32[512,1,24]{2,1,0:T(1,128)S(1)} fusion(f32[24,384,512]{1,0,2:T(8,128)S(1)} %bitcast.102, f32[512,384,1]{1,0,2:T(8,128)S(1)} %get-tuple-element.291), kind=kOutput, calls=%fused_computation.4.clone.1 | convolution fusion | flops 56623104 | bytes 19709952 | tf_op jit(solution)/shard_map/while/body/eval_jaxpr/kxb,bx->bk/dot_general | solution.py:61
  209.3 4.2 gather_fusion
  213.7 9.7 %fusion.54 = f32[512,9216]{1,0:T(8,128)S(1)} fusion(f32[9216,128]{1,0:T(8,128)} %get-tuple-element.325, s32[512]{0:T(512)S(1)} %bitcast.112), kind=kOutput, calls=%fused_computation.9.clone.1 | convolution fusion | flops 7247822848 | bytes 23595008 | tf_op jit(solution)/shard_map/while/body/eval_jaxpr/dot_general | solution.py:57
  223.4 4.8 copy.78
  228.3 23.4 %fusion.55 = f32[512,1,24]{2,1,0:T(1,128)S(1)} fusion(f32[24,384,512]{1,0,2:T(8,128)S(1)} %bitcast.102, f32[512,384,1]{1,0,2:T(8,128)S(1)} %get-tuple-element.291), kind=kOutput, calls=%fused_computation.4.clone.1 | convolution fusion | flops 56623104 | bytes 19709952 | tf_op jit(solution)/shard_map/while/body/eval_jaxpr/kxb,bx->bk/dot_general | solution.py:61
  254.7 12.3 %psum.15 = f32[2048]{0:T(1024)S(1)} all-reduce(f32[2048]{0:T(1024)S(1)} %bitcast.124), channel_id=1, replica_groups=mesh['gx'=8,'gy'=16] {'gx'}, use_global_device_ids=true, to_apply=%region_8.10 | all-reduce | flops 2048 | bytes 16384 | tf_op jit(solution)/shard_map/psum | solution.py:148
  267.1 3.5 copy.41
  270.5 3.4 copy.43
  274.0 39.1 %all-reduce.2.cloned.1.call-done = f32[2048,24]{0,1:T(8,128)} async-done(((f32[2048,24]{0,1:T(8,128)}), f32[2048,24]{0,1:T(8,128)}) %all-reduce.2.cloned.1.call-update) | async-done | bytes 196624 | tf_op jit(solution)/shard_map/psum | solution.py:148
  313.1 6.0 %fusion.23 = f32[3,2048,128]{2,1,0:T(8,128)S(1)} fusion(f32[3,8,128]{2,1,0:T(8,128)S(1)} %copy-done, f32[2048,24]{0,1:T(8,128)} %all-reduce.2.cloned.1.call-done, f32[2048]{0:T(1024)S(1)} %psum.15), kind=kOutput, calls=%fused_computation.55 | convolution fusion | flops 75546624 | bytes 3362816 | tf_op jit(solution)/shard_map/svz,vzl->svl/dot_general | solution.py:72
  319.1 5.8 %reshape.66 = f32[2048,3,128]{2,1,0:T(4,128)} reshape(f32[128,16,384]{2,1,0:T(8,128)} %all-to-all-done) | data formatting | bytes 6291456 | tf_op jit(solution)/shard_map/reshape | solution.py:73
  324.9 6.0 %fusion.19 = f32[2048,3,8]{0,2,1:T(8,128)} fusion(f32[3,8,128]{2,1,0:T(8,128)S(1)} %copy-done, f32[3,2048,128]{2,1,0:T(8,128)S(1)} %fusion.23, f32[2048,3,128]{2,1,0:T(4,128)} %reshape.66, f32[2048]{0:T(1024)S(1)} %bitcast.123), kind=kOutput, calls=%fused_computation.51 | convolution fusion | flops 77119488 | bytes 6508544 | tf_op jit(solution)/shard_map/svl,vzl->svz/dot_general | solution.py:75
  331.9 150.3 %while.26 = (s32[]{:T(128)}, f32[9216,128]{1,0:T(8,128)}, f32[384,128]{1,0:T(8,128)S(1)}, f32[4,512,24]{1,0,2:T(4,128)S(1)}, s32[4,512]{1,0:T(4,128)}, /*index=5...) while((s32[]{:T(128)}, f32[9216,128]{1,0:T(8,128)}, ...), condition=%wide.region_10.12_spmd.clone, body=%wide.region_9.11_spmd.clone.sunk | while | flops 7557453312 | bytes 90326136 | solution.py:115
  333.0 4.2 gather_fusion.1
  340.6 7.5 %copy.82 = f32[64,8,24,384]{3,1,2,0:T(8,128)} copy(f32[64,8,24,384]{3,2,1,0:T(8,128)S(1)} %bitcast.104) | data formatting | bytes 37748736 | tf_op jit(solution)/shard_map/while
  348.1 20.3 %convolution_add_fusion.4 = f32[9216,128]{1,0:T(8,128)} fusion(f32[512,9216]{1,0:T(8,128)} %bitcast.101, f32[9216,128]{1,0:T(8,128)} %get-tuple-element.341, pred[]{:T(512)S(6)} %compare.3, s32[512]{0:T(512)S(1)} %bitcast.114), kind=kOutput, calls=%fused_computation.16.clone.1 | convolution fusion | flops 7250182144 | bytes 28313600 | tf_op jit(solution)/shard_map/while/body/eval_jaxpr/dot_general | solution.py:97
  370.0 4.2 gather_fusion.1
  377.6 7.5 %copy.82 = f32[64,8,24,384]{3,1,2,0:T(8,128)} copy(f32[64,8,24,384]{3,2,1,0:T(8,128)S(1)} %bitcast.104) | data formatting | bytes 37748736 | tf_op jit(solution)/shard_map/while
  385.1 20.9 %convolution_add_fusion.4 = f32[9216,128]{1,0:T(8,128)} fusion(f32[512,9216]{1,0:T(8,128)} %bitcast.101, f32[9216,128]{1,0:T(8,128)} %get-tuple-element.341, pred[]{:T(512)S(6)} %compare.3, s32[512]{0:T(512)S(1)} %bitcast.114), kind=kOutput, calls=%fused_computation.16.clone.1 | convolution fusion | flops 7250182144 | bytes 28313600 | tf_op jit(solution)/shard_map/while/body/eval_jaxpr/dot_general | solution.py:97
  407.7 4.2 gather_fusion.1
  413.0 2.3 broadcast_multiply_fusion.2
  415.3 7.5 %copy.82 = f32[64,8,24,384]{3,1,2,0:T(8,128)} copy(f32[64,8,24,384]{3,2,1,0:T(8,128)S(1)} %bitcast.104) | data formatting | bytes 37748736 | tf_op jit(solution)/shard_map/while
  422.7 20.9 %convolution_add_fusion.4 = f32[9216,128]{1,0:T(8,128)} fusion(f32[512,9216]{1,0:T(8,128)} %bitcast.101, f32[9216,128]{1,0:T(8,128)} %get-tuple-element.341, pred[]{:T(512)S(6)} %compare.3, s32[512]{0:T(512)S(1)} %bitcast.114), kind=kOutput, calls=%fused_computation.16.clone.1 | convolution fusion | flops 7250182144 | bytes 28313600 | tf_op jit(solution)/shard_map/while/body/eval_jaxpr/dot_general | solution.py:97
  445.4 4.2 gather_fusion.1
  452.9 7.5 %copy.82 = f32[64,8,24,384]{3,1,2,0:T(8,128)} copy(f32[64,8,24,384]{3,2,1,0:T(8,128)S(1)} %bitcast.104) | data formatting | bytes 37748736 | tf_op jit(solution)/shard_map/while
  460.4 20.9 %convolution_add_fusion.4 = f32[9216,128]{1,0:T(8,128)} fusion(f32[512,9216]{1,0:T(8,128)} %bitcast.101, f32[9216,128]{1,0:T(8,128)} %get-tuple-element.341, pred[]{:T(512)S(6)} %compare.3, s32[512]{0:T(512)S(1)} %bitcast.114), kind=kOutput, calls=%fused_computation.16.clone.1 | convolution fusion | flops 7250182144 | bytes 28313600 | tf_op jit(solution)/shard_map/while/body/eval_jaxpr/dot_general | solution.py:97
  482.3 25.3 %fusion.11 = f32[3,8,384,128]{3,2,1,0:T(8,128)} fusion(f32[3,8,384,128]{3,2,1,0:T(8,128)} %bitcast.108, f32[3,1,384,128]{3,2,1,0:T(8,128)} %get-tuple-element.195, f32[3,7,384,128]{3,2,1,0:T(8,128)} %get-tuple-element.197, f32[3,7,384,128]{3,2,1,0:T(8,128)} %get-tuple-element.196, f32[3,1,384,128]{3,2,1,0:T(8,128)} %get-tuple-element.194, ...), kind=kLoop, calls=%fused_computation.45 | loop fusion | flops 37748736 | bytes 27033984 | tf_op jit(solution)/shard_map/add | solution.py:152
  (138 shorter events, 44.8 us)
Async XLA Ops:
  6.5 306.6 %copy-start = (f32[3,8,128]{2,1,0:T(8,128)S(1)}, f32[3,8,128]{2,1,0:T(8,128)}, u32[]{:S(2)}) copy-start(f32[3,8,128]{2,1,0:T(8,128)} %param.19) | copy-start | bytes 36868
  11.9 51.3 %all-to-all-start.1 = ((s32[128,16,3]{1,2,0:T(4,128)}), s32[128,16,3]{1,2,0:T(4,128)S(1)}, u32[]{:S(2)}, u32[]{:S(2)}) async-start(s32[128,16,3]{1,2,0:T(4,128)} %copy.46), calls=%async_computation.1 | async-start | bytes 524288 | tf_op jit(solution)/shard_map/all_to_all | solution.py:143
  23.7 18.0 %collective-permute-start = (f32[3,8,1,128]{3,2,1,0:T(1,128)S(1)}, f32[3,8,1,128]{3,2,1,0:T(1,128)S(1)}, u32[]{:S(2)}, u32[]{:S(2)}) collective-permute-start(f32[3,8,1,128]{3,2,1,0:T(1,128)S(1)} %get-tuple-element.193), channel_id=1, source_target_pairs={{16,0},{32,16},{48,32},{64,48},{80,64},{96,80},{112,96},{17,1},{33... | collective-permute-start | bytes 36872 | tf_op jit(solution)/shard_map/ppermute | solution.py:24
  25.9 11.2 %slice-start = ((s8[4718592]{0:T(1024)(128)(4,1)}), s8[4194304]{0:T(1024)(128)(4,1)S(1)}, s32[]{:S(2)}) async-start(s8[4718592]{0:T(1024)(128)(4,1)} %bitcast.106), calls=%async_computation.3 | async-start | bytes 8388608
  25.9 11.2 %slice-start.1 = ((s8[4718592]{0:T(1024)(128)(4,1)}), s8[524288]{0:T(1024)(128)(4,1)S(1)}, s32[]{:S(2)}) async-start(s8[4718592]{0:T(1024)(128)(4,1)} %bitcast.106), calls=%async_computation.4 | async-start | bytes 1048576
  26.0 15.7 %collective-permute-start.1 = (f32[3,8,1,128]{3,2,1,0:T(1,128)S(1)}, f32[3,8,1,128]{3,2,1,0:T(1,128)S(1)}, u32[]{:S(2)}, u32[]{:S(2)}) collective-permute-start(f32[3,8,1,128]{3,2,1,0:T(1,128)S(1)} %get-tuple-element.192), channel_id=1, source_target_pairs={{0,16},{16,32},{32,48},{48,64},{64,80},{80,96},{96,112},{1,17},{17... | collective-permute-start | bytes 36872 | tf_op jit(solution)/shard_map/ppermute | solution.py:23
  41.7 2.7 copy-start.6
  41.7 2.7 copy-start.7
  53.8 213.3 %collective-permute-start.2 = (f32[3,8,386,1]{2,1,3,0:T(8,128)S(1)}, f32[3,8,386,1]{2,1,3,0:T(8,128)S(1)}, u32[]{:S(2)}, u32[]{:S(2)}) collective-permute-start(f32[3,8,386,1]{2,1,3,0:T(8,128)S(1)} %copy.40), channel_id=1, source_target_pairs={{1,0},{2,1},{3,2},{4,3},{5,4},{6,5},{7,6},{8,7},{9,8},{10,9},{11,1... | collective-permute-start | bytes 111176 | tf_op jit(solution)/shard_map/ppermute | solution.py:24
  60.0 210.5 %collective-permute-start.3 = (f32[3,8,386,1]{2,1,3,0:T(8,128)S(1)}, f32[3,8,386,1]{2,1,3,0:T(8,128)S(1)}, u32[]{:S(2)}, u32[]{:S(2)}) collective-permute-start(f32[3,8,386,1]{2,1,3,0:T(8,128)S(1)} %copy.42), channel_id=1, source_target_pairs={{0,1},{1,2},{2,3},{3,4},{4,5},{5,6},{6,7},{7,8},{8,9},{9,10},{10,1... | collective-permute-start | bytes 111176 | tf_op jit(solution)/shard_map/ppermute | solution.py:23
  65.0 254.1 %all-to-all-start = ((f32[128,16,384]{2,1,0:T(8,128)}), f32[128,16,384]{2,1,0:T(8,128)}, u32[]{:S(2)}, u32[]{:S(2)}) async-start(f32[128,16,384]{2,1,0:T(8,128)} %bitcast.12), calls=%async_computation | async-start | bytes 6291456 | tf_op jit(solution)/shard_map/all_to_all | solution.py:136
  76.8 236.3 %all-reduce.2.cloned.1.call-start = ((), (), s32[]{:S(2)}) async-start(), calls=%async_computation.2 | async-start | bytes 393216 | tf_op jit(solution)/shard_map/psum | solution.py:148
  253.3 20.7 %copy-start.4 = (s32[4,512]{1,0:T(4,128)}, s32[4,512]{1,0:T(4,128)S(1)}, u32[]{:S(2)}) copy-start(s32[4,512]{1,0:T(4,128)S(1)} %get-tuple-element.367) | copy-start | bytes 24580
  253.3 20.7 %copy-start.5 = (s32[4,512]{1,0:T(4,128)}, s32[4,512]{1,0:T(4,128)S(1)}, u32[]{:S(2)}) copy-start(s32[4,512]{1,0:T(4,128)S(1)} %get-tuple-element.368) | copy-start | bytes 24580
  324.9 7.1 %copy-start.2 = (f32[384,128]{1,0:T(8,128)S(1)}, f32[384,128]{1,0:T(8,128)}, u32[]{:S(2)}) copy-start(f32[384,128]{1,0:T(8,128)} %custom-call.1) | copy-start | bytes 589828
  331.9 150.4 %copy-start.3 = (f32[8,384,128]{2,1,0:T(8,128)S(1)}, f32[8,384,128]{2,1,0:T(8,128)}, u32[]{:S(2)}) copy-start(f32[8,384,128]{2,1,0:T(8,128)} %get-tuple-element.190) | copy-start | bytes 4718596
  482.3 25.4 %copy-start.1 = (f32[3,8,128]{2,1,0:T(8,128)S(1)}, f32[3,8,128]{2,1,0:T(8,128)}, u32[]{:S(2)}) copy-start(f32[3,8,128]{2,1,0:T(8,128)} %param.19) | copy-start | bytes 36868
Sparse Core Ops, SparseCore 0:
  254.2 58.8 all-reduce.1
where the time goes:
time: 524 us; the launch traced here: 515 us
  matrix products  231 us (44%)
  local copies, waits for them, and re-layouts  141 us (27%)
  other arithmetic  42.4 us (8%)
  waiting for transfers between devices  39.1 us (7%)
  starting transfers between devices  33.7 us (6%)
  between operations  14 us (3%)
  blocking collectives  12.3 us (2%)
    dot_general x4, matrix products, column_per_block(): jnp.einsum('kxb,bx->bk', picked, weight, precision=lax.Precision.HIGHEST)  93.5 us
    dot_general x4, matrix products, spread_per_block(): lax.dot_general(weighted, picker, (((0,), (0,)), ((), ())), precision=lax...  83.1 us
    while x8, local copies, waits for them, and re-layouts  49.2 us
    psum x1, waiting for transfers between devices, local(): summed, totals = lax.psum((colsum, row_parts), 'gx')  39.1 us
    dot_general x4, matrix products, column_per_block(): lax.dot_general(flattened, picker, (((1,), (1,)), ((), ())), precision=la...  38.8 us
    add x1, other arithmetic, local(): return model_state + time_step * (tendency(padded) + nudge_gain * nudge)  25.3 us
    gather x4, local copies, waits for them, and re-layouts, column_per_block(): weight = jnp.take(cressman, x_cells, axis=0)  16.6 us
    gather x4, local copies, waits for them, and re-layouts, spread_per_block(): weight = jnp.take(cressman, x_cells, axis=0) * validity[:, None]  16.6 us
  transfers between devices with their start and end apart: 7, of which 1 were waited for; matrix products, arithmetic and copies ran while one was open for 43% of the time, Pallas kernels for 0%

commit v1 on v0

v1 whole, which is shorter than its diff:
```python
import functools

import jax
import jax.numpy as jnp
from jax import lax
from jax.experimental import pallas as pl
from jax.experimental.pallas import tpu as pltpu
from jax.sharding import PartitionSpec as P

F32 = jnp.float32
BF16 = jnp.bfloat16
I32 = jnp.int32
HIGHEST = lax.Precision.HIGHEST
MESH = pl.DeviceIdType.MESH

advect_coef = 0.5
diffuse_h = 0.2
diffuse_z = 0.1
time_step = 0.5
nudge_gain = 1.0
spread_gain = 0.125

FEATURES = 32
GROUPS = 8
BLOCK = 128


def iota(shape, dim):
    return lax.broadcasted_iota(I32, shape, dim)


def dot(a, b, precision=None):
    return lax.dot_general(
        a, b, (((1,), (0,)), ((), ())), precision=precision, preferred_element_type=F32
    )


def dot_t(a, b, precision=None):
    return lax.dot_general(
        a, b, (((1,), (1,)), ((), ())), precision=precision, preferred_element_type=F32
    )


def split(value):
    high = value.astype(BF16)
    return high, (value - high.astype(F32)).astype(BF16)


def regroup(parts):
    lane_block = iota(parts[0].shape, 1) // 16
    for bit in (1, 2, 4):
        upper = (lane_block & bit) != 0
        out = list(parts)
        for a in range(8):
            if a & bit:
                continue
            low, high = parts[a], parts[a | bit]
            out[a] = jnp.where(upper, pltpu.roll(high, 16 * bit, 1), low)
            out[a | bit] = jnp.where(upper, high, pltpu.roll(low, 128 - 16 * bit, 1))
        parts = out
    return parts


def dispatch_kernel(
    nx, ny, obs_ref, owner_ref, x_ref, y_ref, vert_ref, state_ref,
    at_ref, xi_ref, yi_ref, pos_ref, cnt_ref, nb_ref, base_ref, xh_ref, yh_ref,
    plane, sb, rb, mb, rows, xe, ye, xr, yr,
    load_sem, s1_send, s1_recv, s2_send, s2_recv, h_send, h_recv,
):
    i, j = lax.axis_index("gx"), lax.axis_index("gy")
    load = pltpu.make_async_copy(state_ref, plane, load_sem)
    load.start()
    barrier = pltpu.get_barrier_semaphore()
    for d in range(1, ny):
        pl.semaphore_signal(
            barrier, inc=1, device_id=(i, lax.rem(j + d, ny)), device_id_type=MESH
        )
    for d in range(1, nx):
        pl.semaphore_signal(
            barrier, inc=1, device_id=(lax.rem(i + d, nx), j), device_id_type=MESH
        )

    recs = obs_ref.shape[0]
    planes, tile_x, lanes = plane.shape
    slots = sb.shape[0]
    cap = slots // ny
    vert = vert_ref[...]
    var = iota((planes, lanes), 0) // 8
    basis = jnp.concatenate([jnp.where(var == v, vert, 0.0) for v in range(3)], axis=1)
    basis = jnp.concatenate([basis, jnp.zeros((lanes - planes, 3 * lanes), F32)], axis=0)
    payload = dot_t(obs_ref[...], basis, HIGHEST)
    eye = iota((recs, recs), 0) == iota((recs, recs), 1)
    x_col = jnp.sum(jnp.where(eye, x_ref[...].astype(F32), 0.0), axis=1, keepdims=True)
    y_col = jnp.sum(jnp.where(eye, y_ref[...].astype(F32), 0.0), axis=1, keepdims=True)
    lane = iota((recs, lanes), 1)
    payload = jnp.where(lane == 24, x_col, payload)
    payload = jnp.where(lane == 25, y_col, payload)
    payload = jnp.where(lane == 26, 1.0, payload)
    owner = owner_ref[...]
    onehot = jnp.where(owner == lane, 1.0, 0.0)
    earlier = jnp.where(iota((recs, recs), 0) > iota((recs, recs), 1), 1.0, 0.0)
    rank = jnp.sum(dot(earlier, onehot) * onehot, axis=1, keepdims=True)
    slot = owner.astype(F32) * cap + rank
    slot_row = jnp.sum(jnp.where(eye, slot, 0.0), axis=0, keepdims=True).astype(I32)
    place = jnp.where(iota((slots, recs), 0) == slot_row, 1.0, 0.0)
    sb[...] = dot(place, payload, HIGHEST)

    pl.semaphore_wait(barrier, nx + ny - 2)
    first = []
    for d in range(1, ny):
        c = lax.rem(j + d, ny)
        copy = pltpu.make_async_remote_copy(
            src_ref=sb.at[pl.ds(pl.multiple_of(c * cap, cap), cap)],
            dst_ref=rb.at[pl.ds(pl.multiple_of(j * cap, cap), cap)],
            send_sem=s1_send.at[d], recv_sem=s1_recv.at[d],
            device_id=(i, c), device_id_type=MESH,
        )
        copy.start()
        first.append(copy)
    own = pl.ds(pl.multiple_of(j * cap, cap), cap)
    rb[own, :] = sb[own, :]

    load.wait()
    for k in range(planes):
        xe[0, k : k + 1, :] = plane[k, tile_x - 1 : tile_x, :]
        xe[1, k : k + 1, :] = plane[k, 0:1, :]
    edge_lane = iota((tile_x, lanes), 1)

    def gather_edges(k, edges):
        turned = pltpu.roll(plane[k], 2 * k + 1, 1)
        return jnp.where(edge_lane // 2 == k, turned, edges)

    edges = lax.fori_loop(0, planes, gather_edges, jnp.zeros((tile_x, lanes), F32))
    ye[...] = edges.T[: 2 * planes]
    halo = []
    for n, (src, dst, to) in enumerate((
        (xe.at[0], xr.at[0], (lax.rem(i + 1, nx), j)),
        (xe.at[1], xr.at[1], (lax.rem(i + nx - 1, nx), j)),
        (ye, yr.at[0], (i, lax.rem(j + 1, ny))),
        (ye, yr.at[1], (i, lax.rem(j + ny - 1, ny))),
    )):
        copy = pltpu.make_async_remote_copy(
            src_ref=src, dst_ref=dst, send_sem=h_send.at[n], recv_sem=h_recv.at[n],
            device_id=to, device_id_type=MESH,
        )
        copy.start()
        halo.append(copy)

    for copy in first:
        copy.wait()
    got = rb[...]
    got_t = got.T[:FEATURES]
    valid = got[:, 26:27]
    before = jnp.where(iota((slots, slots), 0) > iota((slots, slots), 1), 1.0, 0.0)
    rank = dot(before, jnp.broadcast_to(valid, (slots, lanes)))[:, 0:1]
    place = jnp.where(
        (iota((slots, slots), 1) == rank.astype(I32)) & (valid > 0.5), 1.0, 0.0
    )
    compact = dot(got_t, place, HIGHEST)
    at_ref[...] = compact
    mb[i] = compact[24:32]
    second = []
    for d in range(1, nx):
        copy = pltpu.make_async_remote_copy(
            src_ref=mb.at[i], dst_ref=mb.at[i],
            send_sem=s2_send.at[d], recv_sem=s2_recv.at[d],
            device_id=(lax.rem(i + d, nx), j), device_id_type=MESH,
        )
        copy.start()
        second.append(copy)
    for copy in halo:
        copy.wait()
    xh_ref[0] = jnp.where(i > 0, xr[0], 0.0)
    xh_ref[1] = jnp.where(i < nx - 1, xr[1], 0.0)
    even = iota((2 * planes, tile_x), 0) % 2 == 0
    south = jnp.where(j > 0, yr[0], 0.0)
    north = jnp.where(j < ny - 1, yr[1], 0.0)
    yh_ref[...] = jnp.where(even, south, north)
    for copy in second:
        copy.wait()

    for k in range(nx):
        for f in range(3):
            rows[f, k : k + 1, :] = mb[k, f : f + 1, :]
    y_cells = rows[1].astype(I32)
    valid = rows[2] > 0.5
    group = jnp.where(valid, y_cells // (lanes // GROUPS), GROUPS)
    masks = jnp.concatenate(
        [jnp.where(group == g, 1.0, 0.0) for g in range(GROUPS)], axis=0
    )
    lines = GROUPS * nx
    after = jnp.where(iota((slots, slots), 0) < iota((slots, slots), 1), 1.0, 0.0)
    rank = dot(masks, after)
    total = jnp.broadcast_to(jnp.sum(masks, axis=1, keepdims=True), (lines, lanes))
    line, other = iota((lines, lines), 0), iota((lines, lines), 1)
    same = line // nx == other // nx
    offset = dot(jnp.where(same & (other < line), 1.0, 0.0), total, HIGHEST)
    whole = dot(jnp.where(same, 1.0, 0.0), total, HIGHEST)
    count = (whole.astype(I32) + (BLOCK - 1)) // BLOCK
    base = dot(
        jnp.where((other // nx < line // nx) & (other % nx == 0), 1.0, 0.0),
        count.astype(F32),
        HIGHEST,
    )
    placed = masks * (base[:, 0:1] * BLOCK + offset[:, 0:1] + rank)
    pos = placed[0:nx]
    for g in range(1, GROUPS):
        pos = pos + placed[g * nx : (g + 1) * nx]
    dump = (slots * nx // BLOCK + GROUPS) * BLOCK
    pos_ref[...] = jnp.where(valid, pos.astype(I32), dump)
    xi_ref[...] = rows[0].astype(I32)
    yi_ref[...] = y_cells % (lanes // GROUPS)
    cnt_ref[...] = jnp.broadcast_to(
        jnp.sum(rows[2], axis=1, keepdims=True), (nx, lanes)
    ).astype(I32)
    nb_ref[...] = count
    base_ref[...] = base.astype(I32)


def gather_kernel(
    nx, xi, yi, pos, cnt, nb, base, cress_hbm, state_hbm,
    part_ref, wt_hi_ref, wt_lo_ref,
    cress, plane, sorted_w, sorted_y, st_hi, st_lo, sums, by_slot, sem,
):
    slots = xi.shape[1]
    planes, tile_x, lanes = plane.shape
    load_w = pltpu.make_async_copy(cress_hbm, cress, sem.at[0])
    load_s = pltpu.make_async_copy(state_hbm, plane, sem.at[1])
    load_w.start()
    load_s.start()
    for g in range(GROUPS):
        blocks = nb[g * nx, 0]

        @pl.when(blocks > 0)
        def _():
            start = pl.multiple_of((base[g * nx, 0] + blocks - 1) * BLOCK, BLOCK)
            sorted_w[pl.ds(start, BLOCK), :] = jnp.zeros((BLOCK, tile_x), F32)
            sorted_y[pl.ds(start, BLOCK), :] = jnp.full((BLOCK, lanes), -1, I32)

    load_w.wait()
    for k in range(nx):

        def bring(n, carry):
            for m in range(8):
                s = n * 8 + m
                p = pos[k, s]
                sorted_w[pl.ds(p, 1), :] = cress[pl.ds(xi[k, s], 1), :]
                sorted_y[pl.ds(p, 1), :] = jnp.full((1, lanes), yi[k, s], I32)
            return carry

        lax.fori_loop(0, (cnt[k, 0] + 7) // 8, bring, 0)

    load_s.wait()
    chunk = 32

    def regroup_chunk(n, carry):
        where = pl.ds(pl.multiple_of(n * chunk, chunk), chunk)
        for v in range(3):
            parts = regroup([plane[v * 8 + z, where, :] for z in range(8)])
            for g in range(GROUPS):
                high, low = split(parts[g])
                st_hi[g, where, v * lanes : (v + 1) * lanes] = high
                st_lo[g, where, v * lanes : (v + 1) * lanes] = low
        return carry

    lax.fori_loop(0, tile_x // chunk, regroup_chunk, 0)

    wide = 3 * lanes
    yy = iota((BLOCK, wide), 1) % 16
    fold = jnp.where(iota((wide, lanes), 0) // 16 == iota((wide, lanes), 1), 1.0, 0.0).astype(BF16)
    lane = iota((BLOCK, lanes), 1)

    def group_sums(g, carry):
        first = base[g * nx, 0]

        def block_sums(b, carry):
            where = pl.ds(pl.multiple_of((first + b) * BLOCK, BLOCK), BLOCK)
            w = sorted_w[where, :]
            high, low = split(w)
            s_hi, s_lo = st_hi[g], st_lo[g]
            products = dot(high, s_hi) + dot(high, s_lo) + dot(low, s_hi)
            y_here = sorted_y[where, :]
            y_wide = jnp.concatenate([y_here, y_here, y_here], axis=1)
            p_hi, p_lo = split(jnp.where(yy == y_wide, products, 0.0))
            colsum = dot(p_hi, fold) + dot(p_lo, fold)
            total = jnp.sum(w, axis=1, keepdims=True)
            sums[where, :] = jnp.where(lane == 24, total, colsum)
            t_hi, t_lo = split(w.T)
            wt_hi_ref[:, where] = t_hi
            wt_lo_ref[:, where] = t_lo
            return carry

        return lax.fori_loop(0, nb[g * nx, 0], block_sums, carry)

    lax.fori_loop(0, GROUPS, group_sums, 0)

    by_slot[...] = jnp.zeros(by_slot.shape, F32)
    for k in range(nx):

        def give(n, carry):
            for m in range(8):
                s = n * 8 + m
                by_slot[pl.ds(k * slots + s, 1), :] = sums[pl.ds(pos[k, s], 1), :]
            return carry

        lax.fori_loop(0, (cnt[k, 0] + 7) // 8, give, 0)
        part_ref[k] = by_slot[k * slots : (k + 1) * slots, :].T[:FEATURES]


def reduce_kernel(
    nx, part_ref, at_ref, vert_ref, out_ref, rs, ag, send1, recv1, send2, recv2
):
    i, j = lax.axis_index("gx"), lax.axis_index("gy")
    barrier = pltpu.get_barrier_semaphore()
    for d in range(1, nx):
        pl.semaphore_signal(
            barrier, inc=1, device_id=(lax.rem(i + d, nx), j), device_id_type=MESH
        )
    pl.semaphore_wait(barrier, nx - 1)
    copies = []
    for d in range(1, nx):
        k = lax.rem(i + d, nx)
        copy = pltpu.make_async_remote_copy(
            src_ref=part_ref.at[k], dst_ref=rs.at[i],
            send_sem=send1.at[d], recv_sem=recv1.at[d],
            device_id=(k, j), device_id_type=MESH,
        )
        copy.start()
        copies.append(copy)
    rs[i] = part_ref[i]
    lanes = vert_ref.shape[1]
    vert = jnp.concatenate([vert_ref[...], jnp.zeros((8, lanes), F32)], axis=0)
    same = iota((FEATURES, FEATURES), 0) // 8 == iota((FEATURES, FEATURES), 1) // 8
    gram = jnp.where(same, dot_t(vert, vert, HIGHEST), 0.0)
    at = at_ref[...]
    row = iota(at.shape, 0)
    for copy in copies:
        copy.wait()
    total = rs[0]
    for k in range(1, nx):
        total = total + rs[k]
    weight = total[24:25, :]
    mean = jnp.where(row < 24, total / jnp.where(weight > 0.0, weight, 1.0), 0.0)
    spread = spread_gain * (at - dot(gram, mean, HIGHEST))
    ag[i] = jnp.where(row < 24, spread, at)
    copies = []
    for d in range(1, nx):
        copy = pltpu.make_async_remote_copy(
            src_ref=ag.at[i], dst_ref=ag.at[i],
            send_sem=send2.at[d], recv_sem=recv2.at[d],
            device_id=(lax.rem(i + d, nx), j), device_id_type=MESH,
        )
        copy.start()
        copies.append(copy)
    for copy in copies:
        copy.wait()
    out_ref[...] = ag[...]


def update_kernel(
    nx, pos, cnt, nb, base, spread_ref, xh_ref, yh_ref, wt_hi_hbm, wt_lo_hbm, state_hbm,
    out_ref, plane, wt_hi, wt_lo, by_slot, sorted_s, halo, nudge, num, weights, sem,
):
    slots = spread_ref.shape[2]
    planes, padded_x, lanes = plane.shape
    tile_x = padded_x - 16
    load_s = pltpu.make_async_copy(state_hbm, plane.at[:, 8 : 8 + tile_x, :], sem.at[0])
    load_h = pltpu.make_async_copy(wt_hi_hbm, wt_hi, sem.at[1])
    load_l = pltpu.make_async_copy(wt_lo_hbm, wt_lo, sem.at[2])
    load_h.start()
    load_l.start()
    load_s.start()
    for g in range(GROUPS):
        blocks = nb[g * nx, 0]

        @pl.when(blocks > 0)
        def _():
            start = pl.multiple_of((base[g * nx, 0] + blocks - 1) * BLOCK, BLOCK)
            sorted_s[pl.ds(start, BLOCK), :] = jnp.full((BLOCK, lanes), -1.0, F32)

    pad = jnp.zeros((lanes - FEATURES, slots), F32)
    for k in range(nx):
        by_slot[k * slots : (k + 1) * slots, :] = jnp.concatenate(
            [spread_ref[k], pad], axis=0
        ).T

        def bring(n, carry):
            for m in range(8):
                s = n * 8 + m
                sorted_s[pl.ds(pos[k, s], 1), :] = by_slot[pl.ds(k * slots + s, 1), :]
            return carry

        lax.fori_loop(0, (cnt[k, 0] + 7) // 8, bring, 0)

    halo[...] = jnp.concatenate(
        [yh_ref[...], jnp.zeros((lanes - 2 * planes, tile_x), F32)], axis=0
    ).T

    wide = 3 * lanes
    yy = iota((BLOCK, wide), 1) % 16
    widen = jnp.where(iota((lanes, wide), 1) // 16 == iota((lanes, wide), 0), 1.0, 0.0).astype(BF16)
    load_h.wait()
    load_l.wait()

    def group_update(g, carry):
        first = base[g * nx, 0]
        num[...] = jnp.zeros(num.shape, F32)
        weights[...] = jnp.zeros(weights.shape, F32)

        def block_update(b, carry):
            where = pl.ds(pl.multiple_of((first + b) * BLOCK, BLOCK), BLOCK)
            value = sorted_s[where, :]
            y_here = (value[:, 25:26] + 0.5).astype(I32)
            match = (value[:, 25:26] > -0.5) & (yy == y_here % 16)
            high, low = split(value)
            s_hi = jnp.where(match, dot(high, widen), 0.0).astype(BF16)
            s_lo = jnp.where(match, dot(low, widen), 0.0).astype(BF16)
            ones = jnp.where(match[:, :lanes], 1.0, 0.0).astype(BF16)
            w_hi, w_lo = wt_hi[:, where], wt_lo[:, where]
            num[...] += dot(w_hi, s_hi) + dot(w_hi, s_lo) + dot(w_lo, s_hi)
            weights[...] += dot(w_hi, ones) + dot(w_lo, ones)
            return carry

        lax.fori_loop(0, nb[g * nx, 0], block_update, 0)
        scale = 1.0 / jnp.maximum(weights[...], 1.0)
        for v in range(3):
            nudge[g, :, v * lanes : (v + 1) * lanes] = num[:, v * lanes : (v + 1) * lanes] * scale
        return carry

    lax.fori_loop(0, GROUPS, group_update, 0)

    load_s.wait()
    for k in range(planes):
        plane[k, 7:8, :] = xh_ref[0, k : k + 1, :]
        plane[k, 8 + tile_x : 9 + tile_x, :] = xh_ref[1, k : k + 1, :]

    chunk = 16
    lane = iota((chunk, lanes), 1)

    def finish(n, carry):
        start = pl.multiple_of(n * chunk, chunk)
        edges = halo[pl.ds(start, chunk), :]
        centers = []
        for k in range(planes):
            centers.append(plane[k, pl.ds(pl.multiple_of(start + 8, 8), chunk), :])
        for v in range(3):
            gains = regroup(
                [nudge[g, pl.ds(start, chunk), v * lanes : (v + 1) * lanes] for g in range(GROUPS)]
            )
            for z in range(8):
                k = v * 8 + z
                center = centers[k]
                window = plane[k, pl.ds(start, chunk + 16), :]
                west = window[7 : 7 + chunk]
                east = window[9 : 9 + chunk]
                beside = pltpu.roll(edges, (lanes - 1 - 2 * k) % lanes, 1)
                south = pltpu.roll(jnp.where(lane == lanes - 1, beside, center), 1, 1)
                north = pltpu.roll(jnp.where(lane == 0, beside, center), lanes - 1, 1)
                upper = centers[v * 8 + min(z + 1, 7)]
                lower = centers[v * 8 + max(z - 1, 0)]
                wind_u, wind_v = centers[z], centers[8 + z]
                advection = (-0.5 * advect_coef) * (
                    wind_u * (east - west) + wind_v * (north - south)
                )
                laplace = east + west + north + south - 4.0 * center
                tendency = (
                    advection + diffuse_h * laplace + diffuse_z * (upper + lower - 2.0 * center)
                )
                out_ref[k, pl.ds(start, chunk), :] = center + time_step * (
                    tendency + nudge_gain * gains[z]
                )
        return carry

    lax.fori_loop(0, tile_x // chunk, finish, 0)


VM = pltpu.MemorySpace.VMEM


def vmem():
    return pl.BlockSpec(memory_space=VM)


def smem():
    return pl.BlockSpec(memory_space=pltpu.MemorySpace.SMEM)


def hbm():
    return pl.BlockSpec(memory_space=pl.ANY)


def local(nx, ny, model_state, obs_val, obs_owner, obs_x, obs_y, cressman, vertical):
    fields, levels, tile_x, lanes = model_state.shape
    planes = fields * levels
    recs = obs_val.shape[0]
    cap = max(2, 2 * recs // ny)
    slots = ny * cap
    rows = (slots * nx // BLOCK + GROUPS) * BLOCK
    state = model_state.reshape(planes, tile_x, lanes)
    vert = vertical.reshape(planes, vertical.shape[2])
    shape = jax.ShapeDtypeStruct
    dma = pltpu.SemaphoreType.DMA
    limit = 56 * 1024 * 1024

    at, xi, yi, pos, cnt, nb, base, xh, yh = pl.pallas_call(
        functools.partial(dispatch_kernel, nx, ny),
        out_shape=(
            shape((FEATURES, slots), F32),
            shape((nx, slots), I32),
            shape((nx, slots), I32),
            shape((nx, slots), I32),
            shape((nx, lanes), I32),
            shape((GROUPS * nx, lanes), I32),
            shape((GROUPS * nx, lanes), I32),
            shape((2, planes, lanes), F32),
            shape((2 * planes, tile_x), F32),
        ),
        in_specs=[vmem()] * 5 + [hbm()],
        out_specs=[vmem()] * 9,
        scratch_shapes=[
            pltpu.VMEM((planes, tile_x, lanes), F32),
            pltpu.VMEM((slots, lanes), F32),
            pltpu.VMEM((slots, lanes), F32),
            pltpu.VMEM((nx, 8, slots), F32),
            pltpu.VMEM((3, nx, slots), F32),
            pltpu.VMEM((2, planes, lanes), F32),
            pltpu.VMEM((2 * planes, tile_x), F32),
            pltpu.VMEM((2, planes, lanes), F32),
            pltpu.VMEM((2, 2 * planes, tile_x), F32),
            dma,
            dma((ny,)),
            dma((ny,)),
            dma((nx,)),
            dma((nx,)),
            dma((4,)),
            dma((4,)),
        ],
        compiler_params=pltpu.CompilerParams(
            collective_id=0, has_side_effects=True, vmem_limit_bytes=limit
        ),
        name="dispatch",
    )(obs_val, obs_owner, obs_x.reshape(1, recs), obs_y.reshape(1, recs), vert, state)

    part, wt_hi, wt_lo = pl.pallas_call(
        functools.partial(gather_kernel, nx),
        out_shape=(
            shape((nx, FEATURES, slots), F32),
            shape((tile_x, rows), BF16),
            shape((tile_x, rows), BF16),
        ),
        in_specs=[smem()] * 6 + [hbm()] * 2,
        out_specs=[vmem()] * 3,
        scratch_shapes=[
            pltpu.VMEM(cressman.shape, F32),
            pltpu.VMEM((planes, tile_x, lanes), F32),
            pltpu.VMEM((rows + 8, tile_x), F32),
            pltpu.VMEM((rows + 8, lanes), I32),
            pltpu.VMEM((GROUPS, tile_x, 3 * lanes), BF16),
            pltpu.VMEM((GROUPS, tile_x, 3 * lanes), BF16),
            pltpu.VMEM((rows + 8, lanes), F32),
            pltpu.VMEM((nx * slots, lanes), F32),
            dma((2,)),
        ],
        compiler_params=pltpu.CompilerParams(vmem_limit_bytes=limit),
        name="column_sums",
    )(xi, yi, pos, cnt, nb, base, cressman, state)

    spread = pl.pallas_call(
        functools.partial(reduce_kernel, nx),
        out_shape=shape((nx, FEATURES, slots), F32),
        in_specs=[vmem()] * 3,
        out_specs=vmem(),
        scratch_shapes=[
            pltpu.VMEM((nx, FEATURES, slots), F32),
            pltpu.VMEM((nx, FEATURES, slots), F32),
            dma((nx,)),
            dma((nx,)),
            dma((nx,)),
            dma((nx,)),
        ],
        compiler_params=pltpu.CompilerParams(
            collective_id=1, has_side_effects=True, vmem_limit_bytes=limit
        ),
        name="innovations",
    )(part, at, vert)

    out = pl.pallas_call(
        functools.partial(update_kernel, nx),
        out_shape=shape((planes, tile_x, lanes), F32),
        in_specs=[smem()] * 4 + [vmem()] * 3 + [hbm()] * 3,
        out_specs=vmem(),
        scratch_shapes=[
            pltpu.VMEM((planes, tile_x + 16, lanes), F32),
            pltpu.VMEM((tile_x, rows), BF16),
            pltpu.VMEM((tile_x, rows), BF16),
            pltpu.VMEM((nx * slots, lanes), F32),
            pltpu.VMEM((rows + 8, lanes), F32),
            pltpu.VMEM((tile_x, lanes), F32),
            pltpu.VMEM((GROUPS, tile_x, 3 * lanes), F32),
            pltpu.VMEM((tile_x, 3 * lanes), F32),
            pltpu.VMEM((tile_x, lanes), F32),
            dma((3,)),
        ],
        compiler_params=pltpu.CompilerParams(vmem_limit_bytes=limit),
        name="update",
    )(pos, cnt, nb, base, spread, xh, yh, wt_hi, wt_lo, state)
    return out.reshape(model_state.shape)


def solution(mesh):
    in_specs = (
        P(None, None, "gx", "gy"),
        P(("gx", "gy"), None),
        P(("gx", "gy"), None),
        P(("gx", "gy")),
        P(("gx", "gy")),
        P(None, "gx"),
        P(),
    )
    out_specs = P(None, None, "gx", "gy")
    return jax.shard_map(
        functools.partial(local, mesh.shape["gx"], mesh.shape["gy"]),
        mesh=mesh, in_specs=in_specs, out_specs=out_specs, check_vma=False,
    )
```

time: 524 us -> 131 us (0.25)
  the two profiles are of different devices: /device:TPU:5 before, /device:TPU:1 now
where the time goes in v1:
time: 131 us
  Pallas kernels  129 us (98%)
  local copies, waits for them, and re-layouts  1.39 us (1%)
    pallas_call x1, Pallas kernels, local(): pl.pallas_call(functools.partial(update_kernel, nx), out_shape=shape((pla...  52.3 us
    pallas_call x1, Pallas kernels, local(): pl.pallas_call(functools.partial(gather_kernel, nx), out_shape=(shape((nx...  42.7 us
    pallas_call x1, Pallas kernels, local(): pl.pallas_call(functools.partial(dispatch_kernel, nx, ny), out_shape=(sha...  20 us
    pallas_call x1, Pallas kernels, local(): pl.pallas_call(functools.partial(reduce_kernel, nx), out_shape=shape((nx,...  14.3 us

profile of v1, /device:TPU:1, one launch (start us, length us, event | category | flops | bytes accessed | tf_op | source)
XLA Modules:
  0.0 130.7 jit_solution(16236572813815103004)
XLA Ops:
  0.0 1.4 %copy.8.owner_ref = s32[128,1]{1,0:T(8,128)} copy(s32[128,1]{0,1:T(1,128)} %param.9) | data formatting | bytes 1024 | tf_op args[2]
  1.4 20.0 %dispatch.1 = (f32[32,256]{1,0:T(8,128)}, s32[8,256]{1,0:T(8,128)}, s32[8,256]{1,0:T(8,128)}, s32[8,256]{1,0:T(8,128)}, s32[8,128]{1,0:T(8,128)}, /*index=5*/s32...) custom-call(f32[128,384]{1,0:T(8,128)} %obs_ref.1, s32[128,1]{1,0:T(8,128)} %copy.8.owner_ref, ...), custom_call_target="tpu_custom_call" | custom-call | tf_op jit(solution)/shard_map/dispatch/pallas_call | solution.py:505
  21.4 42.7 %column_sums.1 = (f32[8,32,256]{2,1,0:T(8,128)}, bf16[384,3072]{1,0:T(8,128)(2,1)}, bf16[384,3072]{1,0:T(8,128)(2,1)}) custom-call(s32[8,256]{1,0:T(8,128)} %get-tuple-element.21.xi, s32[8,256]{1,0:T(8,128)} %get-tuple-element.22.yi, s32[8,256]{1,0:T(8,128)} %get-tuple-element.17.pos, s32[8,128]{1,0:T(8,128)} %get-tuple-element.18.cnt, ...), custom_call_target="tpu_custom_call" | custom-call | tf_op jit(solution)/shard_map/column_sums/pallas_call | solution.py:544
  64.1 14.3 %innovations.1.spread_ref = f32[8,32,256]{2,1,0:T(8,128)} custom-call(f32[8,32,256]{2,1,0:T(8,128)} %get-tuple-element.23.part_ref, f32[32,256]{1,0:T(8,128)} %get-tuple-element.24.at_ref, f32[24,128]{1,0:T(8,128)} %bitcast.9), custom_call_target="tpu_custom_call" | custom-call | tf_op jit(solution)/shard_map/innovations/pallas_call | solution.py:568
  78.4 52.3 %update.1 = f32[24,384,128]{2,1,0:T(8,128)} custom-call(s32[8,256]{1,0:T(8,128)} %get-tuple-element.17.pos, s32[8,128]{1,0:T(8,128)} %get-tuple-element.18.cnt, s32[64,128]{1,0:T(8,128)} %get-tuple-element.19.nb, s32[64,128]{1,0:T(8,128)} %get-tuple-element.20.base, f32[8,32,256]{2,1,0:T(8,128)} %innovations.1.spread_ref, ...), custom_call_target="tpu_custom_call" | custom-call | tf_op jit(solution)/shard_map/update/pallas_call | solution.py:587

commit v2 on v1

v2 whole, which is shorter than its diff:
```python
import functools

import jax
import jax.numpy as jnp
from jax import lax
from jax.experimental import pallas as pl
from jax.experimental.pallas import tpu as pltpu
from jax.sharding import PartitionSpec as P

F32 = jnp.float32
BF16 = jnp.bfloat16
I32 = jnp.int32
HIGHEST = lax.Precision.HIGHEST
MESH = pl.DeviceIdType.MESH

advect_coef = 0.5
diffuse_h = 0.2
diffuse_z = 0.1
time_step = 0.5
nudge_gain = 1.0
spread_gain = 0.125

FEATURES = 32
GROUPS = 8
BLOCK = 128


def iota(shape, dim):
    return lax.broadcasted_iota(I32, shape, dim)


def dot(a, b, precision=None):
    return lax.dot_general(
        a, b, (((1,), (0,)), ((), ())), precision=precision, preferred_element_type=F32
    )


def dot_t(a, b, precision=None):
    return lax.dot_general(
        a, b, (((1,), (1,)), ((), ())), precision=precision, preferred_element_type=F32
    )


def split(value):
    high = value.astype(BF16)
    return high, (value - high.astype(F32)).astype(BF16)


def barrel(parts):
    block = iota(parts[0].shape, 1) // 16
    for bit in (1, 2, 4):
        upper = (block & bit) != 0
        parts = [jnp.where(upper, parts[(c + bit) % 8], parts[c]) for c in range(8)]
    return parts


def to_groups(parts):
    parts = barrel([pltpu.roll(p, 16 * z, 1) if z else p for z, p in enumerate(parts)])
    return [parts[-g % 8] for g in range(8)]


def to_levels(parts):
    parts = barrel(parts)
    return [
        pltpu.roll(parts[-z % 8], 128 - 16 * z, 1) if z else parts[0] for z in range(8)
    ]


def group_of(lane, g):
    return lane // 128 * 8 + (lane // 16 + 8 - g) % 8


def dispatch_kernel(
    nx, ny, obs_ref, owner_ref, x_ref, y_ref, vert_ref, state_hbm,
    at_ref, info_ref, meta_ref, base_hbm, high_hbm, low_hbm,
    plane, moved, st_hi, st_lo, sb, rb, mb, rows, xe, ye, xr, yr,
    load_sem, store_sem, s1_send, s1_recv, s2_send, s2_recv, h_send, h_recv,
):
    i, j = lax.axis_index("gx"), lax.axis_index("gy")
    planes, padded_x, lanes = plane.shape
    tile_x = padded_x - 16
    load = pltpu.make_async_copy(state_hbm, plane.at[:, 8 : 8 + tile_x, :], load_sem)
    load.start()
    barrier = pltpu.get_barrier_semaphore()
    for d in range(1, ny):
        pl.semaphore_signal(
            barrier, inc=1, device_id=(i, lax.rem(j + d, ny)), device_id_type=MESH
        )
    for d in range(1, nx):
        pl.semaphore_signal(
            barrier, inc=1, device_id=(lax.rem(i + d, nx), j), device_id_type=MESH
        )

    recs = obs_ref.shape[0]
    slots = sb.shape[0]
    cap = slots // ny
    vert = vert_ref[...]
    var = iota((planes, lanes), 0) // 8
    basis = jnp.concatenate([jnp.where(var == v, vert, 0.0) for v in range(3)], axis=1)
    basis = jnp.concatenate([basis, jnp.zeros((lanes - planes, 3 * lanes), F32)], axis=0)
    payload = dot_t(obs_ref[...], basis, HIGHEST)
    eye = iota((recs, recs), 0) == iota((recs, recs), 1)
    x_col = jnp.sum(jnp.where(eye, x_ref[...].astype(F32), 0.0), axis=1, keepdims=True)
    y_col = jnp.sum(jnp.where(eye, y_ref[...].astype(F32), 0.0), axis=1, keepdims=True)
    lane = iota((recs, lanes), 1)
    payload = jnp.where(lane == 24, x_col, payload)
    payload = jnp.where(lane == 25, y_col, payload)
    payload = jnp.where(lane == 26, 1.0, payload)
    owner = jnp.sum(jnp.where(eye, owner_ref[...], 0), axis=1, keepdims=True)
    onehot = jnp.where(owner == lane, 1.0, 0.0)
    earlier = jnp.where(iota((recs, recs), 0) > iota((recs, recs), 1), 1.0, 0.0)
    rank = jnp.sum(dot(earlier, onehot) * onehot, axis=1, keepdims=True)
    slot = owner.astype(F32) * cap + rank
    slot_row = jnp.sum(jnp.where(eye, slot, 0.0), axis=0, keepdims=True).astype(I32)
    place = jnp.where(iota((slots, recs), 0) == slot_row, 1.0, 0.0)
    sb[...] = dot(place, payload, HIGHEST)

    pl.semaphore_wait(barrier, nx + ny - 2)
    first = []
    for d in range(1, ny):
        c = lax.rem(j + d, ny)
        copy = pltpu.make_async_remote_copy(
            src_ref=sb.at[pl.ds(pl.multiple_of(c * cap, cap), cap)],
            dst_ref=rb.at[pl.ds(pl.multiple_of(j * cap, cap), cap)],
            send_sem=s1_send.at[d], recv_sem=s1_recv.at[d],
            device_id=(i, c), device_id_type=MESH,
        )
        copy.start()
        first.append(copy)
    own = pl.ds(pl.multiple_of(j * cap, cap), cap)
    rb[own, :] = sb[own, :]

    load.wait()
    for k in range(planes):
        xe[0, k : k + 1, :] = plane[k, 7 + tile_x : 8 + tile_x, :]
        xe[1, k : k + 1, :] = plane[k, 8:9, :]
    edge_lane = iota((tile_x, lanes), 1)

    def gather_edges(k, edges):
        turned = pltpu.roll(plane[k, 8 : 8 + tile_x, :], 2 * k + 1, 1)
        return jnp.where(edge_lane // 2 == k, turned, edges)

    edges = lax.fori_loop(0, planes, gather_edges, jnp.zeros((tile_x, lanes), F32))
    ye[...] = edges.T[: 2 * planes]
    halo = []
    for n, (src, dst, to) in enumerate((
        (xe.at[0], xr.at[0], (lax.rem(i + 1, nx), j)),
        (xe.at[1], xr.at[1], (lax.rem(i + nx - 1, nx), j)),
        (ye, yr.at[0], (i, lax.rem(j + 1, ny))),
        (ye, yr.at[1], (i, lax.rem(j + ny - 1, ny))),
    )):
        copy = pltpu.make_async_remote_copy(
            src_ref=src, dst_ref=dst, send_sem=h_send.at[n], recv_sem=h_recv.at[n],
            device_id=to, device_id_type=MESH,
        )
        copy.start()
        halo.append(copy)

    chunk = 32

    def group_chunk(n, carry):
        start = pl.multiple_of(n * chunk, chunk)
        here = pl.ds(start, chunk)
        for v in range(3):
            parts = to_groups(
                [plane[v * 8 + z, pl.ds(pl.multiple_of(start + 8, 8), chunk), :] for z in range(8)]
            )
            for g in range(GROUPS):
                high, low = split(parts[g])
                st_hi[g, here, v * lanes : (v + 1) * lanes] = high
                st_lo[g, here, v * lanes : (v + 1) * lanes] = low
        return carry

    lax.fori_loop(0, tile_x // chunk, group_chunk, 0)
    stores = [
        pltpu.make_async_copy(st_hi, high_hbm, store_sem.at[0]),
        pltpu.make_async_copy(st_lo, low_hbm, store_sem.at[1]),
    ]
    for copy in stores:
        copy.start()

    for copy in first:
        copy.wait()
    got = rb[...]
    got_t = got.T[:FEATURES]
    valid = got[:, 26:27]
    before = jnp.where(iota((slots, slots), 0) > iota((slots, slots), 1), 1.0, 0.0)
    rank = dot(before, jnp.broadcast_to(valid, (slots, lanes)))[:, 0:1]
    place = jnp.where(
        (iota((slots, slots), 1) == rank.astype(I32)) & (valid > 0.5), 1.0, 0.0
    )
    compact = dot(got_t, place, HIGHEST)
    at_ref[...] = compact
    mb[i] = compact[24:32]
    second = []
    for d in range(1, nx):
        copy = pltpu.make_async_remote_copy(
            src_ref=mb.at[i], dst_ref=mb.at[i],
            send_sem=s2_send.at[d], recv_sem=s2_recv.at[d],
            device_id=(lax.rem(i + d, nx), j), device_id_type=MESH,
        )
        copy.start()
        second.append(copy)
    for copy in halo:
        copy.wait()
    for k in range(planes):
        plane[k, 7:8, :] = jnp.where(i > 0, xr[0, k : k + 1, :], 0.0)
        plane[k, 8 + tile_x : 9 + tile_x, :] = jnp.where(i < nx - 1, xr[1, k : k + 1, :], 0.0)
    even = iota((2 * planes, tile_x), 0) % 2 == 0
    south = jnp.where(j > 0, yr[0], 0.0)
    north = jnp.where(j < ny - 1, yr[1], 0.0)
    beside = jnp.concatenate(
        [jnp.where(even, south, north), jnp.zeros((lanes - 2 * planes, tile_x), F32)], axis=0
    ).T
    beside_high, beside_low = split(beside)
    beside = jnp.where(
        iota((tile_x, lanes), 1) < lanes // 2,
        beside_high.astype(F32),
        pltpu.roll(beside_low.astype(F32), lanes // 2, 1),
    ).astype(BF16)
    near = time_step * diffuse_h
    wind = time_step * 0.5 * advect_coef
    own_part = 1.0 - time_step * (4.0 * diffuse_h + 2.0 * diffuse_z)
    here = pl.ds(8, tile_x)
    source, target = iota((lanes, 2 * lanes), 0), iota((lanes, 2 * lanes), 1)
    turn = (source == target + 1) | ((target >= lanes) & (source == target - lanes - 1))
    turn = jnp.where(turn, 1.0, 0.0).astype(BF16)

    def move(k, carry):
        z = k % 8
        center = plane[k, here, :]
        high, low = split(center)
        fill = ((source % (lanes // 2) == 2 * k + 1) & (target == lanes - 1)) | (
            (source % (lanes // 2) == 2 * k) & (target == lanes)
        )
        fill = jnp.where(fill, 1.0, 0.0).astype(BF16)
        sides = dot(
            jnp.concatenate([high, low, beside], axis=1),
            jnp.concatenate([turn, turn, fill], axis=0),
        )
        wind_u = wind * plane[z, here, :]
        wind_v = wind * plane[8 + z, here, :]
        upper = plane[k + jnp.where(z < 7, 1, 0), here, :]
        lower = plane[k - jnp.where(z > 0, 1, 0), here, :]
        moved[k] = (
            own_part * center
            + (near - wind_u) * plane[k, 9 : 9 + tile_x, :]
            + (near + wind_u) * plane[k, 7 : 7 + tile_x, :]
            + (near - wind_v) * sides[:, :lanes]
            + (near + wind_v) * sides[:, lanes:]
            + (time_step * diffuse_z) * (upper + lower)
        )
        return carry

    lax.fori_loop(0, planes, move, 0)
    stores.append(pltpu.make_async_copy(moved, base_hbm, store_sem.at[2]))
    stores[2].start()
    for copy in second:
        copy.wait()

    for k in range(nx):
        for f in range(3):
            rows[f, k : k + 1, :] = mb[k, f : f + 1, :]
    y_cells = rows[1].astype(I32)
    valid = rows[2] > 0.5
    group = jnp.where(valid, y_cells // (lanes // GROUPS), GROUPS)
    masks = jnp.concatenate(
        [jnp.where(group == g, 1.0, 0.0) for g in range(GROUPS)], axis=0
    )
    lines = GROUPS * nx
    after = jnp.where(iota((slots, slots), 0) < iota((slots, slots), 1), 1.0, 0.0)
    rank = dot(masks, after)
    total = jnp.broadcast_to(jnp.sum(masks, axis=1, keepdims=True), (lines, lanes))
    line, other = iota((lines, lines), 0), iota((lines, lines), 1)
    same = line // nx == other // nx
    offset = dot(jnp.where(same & (other < line), 1.0, 0.0), total, HIGHEST)
    whole = dot(jnp.where(same, 1.0, 0.0), total, HIGHEST)
    count = (whole.astype(I32) + (BLOCK - 1)) // BLOCK
    base = dot(
        jnp.where((other // nx < line // nx) & (other % nx == 0), 1.0, 0.0),
        count.astype(F32),
        HIGHEST,
    )
    placed = masks * (base[:, 0:1] * BLOCK + offset[:, 0:1] + rank)
    pos = placed[0:nx]
    for g in range(1, GROUPS):
        pos = pos + placed[g * nx : (g + 1) * nx]
    dump = (slots * nx // BLOCK + GROUPS + 1) * BLOCK
    info_ref[0:nx, :] = rows[0].astype(I32)
    info_ref[nx : 2 * nx, :] = y_cells % (lanes // GROUPS)
    info_ref[2 * nx : 3 * nx, :] = jnp.where(valid, pos.astype(I32), dump)
    info_ref[3 * nx : 4 * nx, :] = jnp.broadcast_to(
        jnp.sum(rows[2], axis=1, keepdims=True), (nx, slots)
    ).astype(I32)
    base = base.astype(I32)
    for g in range(GROUPS):
        info_ref[4 * nx + g : 4 * nx + g + 1, 0:lanes] = base[g * nx : g * nx + 1, :]
        info_ref[4 * nx + g : 4 * nx + g + 1, lanes : 2 * lanes] = count[g * nx : g * nx + 1, :]
    meta_ref[...] = mb[...]
    for copy in stores:
        copy.wait()


def block_tools(nx, lanes, info):
    def base(g):
        return info[4 * nx + g, 0]

    def count(g):
        return info[4 * nx + g, lanes]

    def group(b):
        found = 0
        for g in range(1, GROUPS):
            found = found + jnp.where(b >= base(g), 1, 0)
        return found

    return base, count, group, base(GROUPS - 1) + count(GROUPS - 1)


def gather_kernel(
    nx, info, cress_hbm, high_hbm, low_hbm, part_ref, wt_hi_hbm, wt_lo_hbm,
    cress, st_hi, st_lo, sorted_w, sorted_y, wt_hi, wt_lo, sums, by_slot, fold, sem,
):
    slots = info.shape[1]
    pieces, _, lanes = cress.shape
    tile_x = pieces * lanes
    base, count, group, blocks = block_tools(nx, lanes, info)
    loads = [
        pltpu.make_async_copy(
            cress_hbm.at[:, c * lanes : (c + 1) * lanes], cress.at[c], sem.at[c]
        )
        for c in range(pieces)
    ]
    state_loads = [
        pltpu.make_async_copy(high_hbm, st_hi, sem.at[3]),
        pltpu.make_async_copy(low_hbm, st_lo, sem.at[4]),
    ]
    for copy in loads + state_loads:
        copy.start()

    def clear(b):
        where = pl.ds(pl.multiple_of(b * BLOCK, BLOCK), BLOCK)
        for c in range(pieces):
            sorted_w[c, where, :] = jnp.zeros((BLOCK, lanes), F32)
        sorted_y[where, :] = jnp.full((BLOCK, lanes), -1, I32)

    for g in range(GROUPS):
        pl.when(count(g) > 0)(functools.partial(clear, base(g) + count(g) - 1))
    clear(blocks)
    wide = 3 * lanes
    for g in range(GROUPS):
        fold[g] = jnp.where(
            group_of(iota((wide, lanes), 0), g) == iota((wide, lanes), 1), 1.0, 0.0
        ).astype(BF16)

    for copy in loads:
        copy.wait()
    for k in range(nx):

        def bring(n, carry):
            at = [n * 8 + m for m in range(8)]
            cells = [info[k, s] for s in at]
            places = [info[2 * nx + k, s] for s in at]
            got = [[cress[c, pl.ds(x, 1), :] for c in range(pieces)] for x in cells]
            for p, found in zip(places, got):
                for c in range(pieces):
                    sorted_w[c, pl.ds(p, 1), :] = found[c]
            for p, s in zip(places, at):
                sorted_y[pl.ds(p, 1), :] = jnp.full((1, lanes), info[nx + k, s], I32)
            return carry

        lax.fori_loop(0, (info[3 * nx + k, 0] + 7) // 8, bring, 0)

    for copy in state_loads:
        copy.wait()
    yy = iota((BLOCK, wide), 1) % 16
    lane = iota((BLOCK, lanes), 1)

    def block_sums(b):
        where = pl.ds(pl.multiple_of(b * BLOCK, BLOCK), BLOCK)
        g = group(b)
        parts = [sorted_w[c, where, :] for c in range(pieces)]
        high, low = split(jnp.concatenate(parts, axis=1))
        both = dot(jnp.concatenate([high, low], axis=0), st_hi[g])
        products = both[:BLOCK] + both[BLOCK:] + dot(high, st_lo[g])
        y_here = sorted_y[where, :]
        y_wide = jnp.concatenate([y_here, y_here, y_here], axis=1)
        chosen = split(jnp.where(yy == y_wide, products, 0.0))
        both = dot(jnp.concatenate(chosen, axis=0), fold[g])
        total = jnp.sum(parts[0] + parts[1] + parts[2], axis=1, keepdims=True)
        result = jnp.where(lane == 24, total, both[:BLOCK] + both[BLOCK:])
        turned = [split(part.T) for part in parts]
        return where, result, turned

    def two_blocks(n, carry):
        for where, result, turned in [block_sums(2 * n), block_sums(2 * n + 1)]:
            sums[where, :] = result
            for c in range(pieces):
                wt_hi[c * lanes : (c + 1) * lanes, where] = turned[c][0]
                wt_lo[c * lanes : (c + 1) * lanes, where] = turned[c][1]
        return carry

    lax.fori_loop(0, (blocks + 1) // 2, two_blocks, 0)
    stores = [
        pltpu.make_async_copy(wt_hi, wt_hi_hbm, sem.at[5]),
        pltpu.make_async_copy(wt_lo, wt_lo_hbm, sem.at[6]),
    ]
    for copy in stores:
        copy.start()

    by_slot[...] = jnp.zeros(by_slot.shape, F32)
    for k in range(nx):

        def give(n, carry):
            start = pl.multiple_of(n * 8, 8)
            got = [sums[pl.ds(info[2 * nx + k, start + m], 1), :] for m in range(8)]
            by_slot[pl.ds(k * slots + start, 8), :] = jnp.concatenate(got, axis=0)
            return carry

        lax.fori_loop(0, (info[3 * nx + k, 0] + 7) // 8, give, 0)
        part_ref[k] = by_slot[k * slots : (k + 1) * slots, :].T[:FEATURES]
    for copy in stores:
        copy.wait()


def reduce_kernel(
    nx, part_ref, at_ref, vert_ref, out_ref, rs, ag, send1, recv1, send2, recv2
):
    i, j = lax.axis_index("gx"), lax.axis_index("gy")
    barrier = pltpu.get_barrier_semaphore()
    for d in range(1, nx):
        pl.semaphore_signal(
            barrier, inc=1, device_id=(lax.rem(i + d, nx), j), device_id_type=MESH
        )
    pl.semaphore_wait(barrier, nx - 1)
    copies = []
    for d in range(1, nx):
        k = lax.rem(i + d, nx)
        copy = pltpu.make_async_remote_copy(
            src_ref=part_ref.at[k], dst_ref=rs.at[i],
            send_sem=send1.at[d], recv_sem=recv1.at[d],
            device_id=(k, j), device_id_type=MESH,
        )
        copy.start()
        copies.append(copy)
    rs[i] = part_ref[i]
    lanes = vert_ref.shape[1]
    vert = jnp.concatenate([vert_ref[...], jnp.zeros((8, lanes), F32)], axis=0)
    same = iota((FEATURES, FEATURES), 0) // 8 == iota((FEATURES, FEATURES), 1) // 8
    gram = jnp.where(same, dot_t(vert, vert, HIGHEST), 0.0)
    at = at_ref[...]
    row = iota(at.shape, 0)
    for copy in copies:
        copy.wait()
    total = rs[0]
    for k in range(1, nx):
        total = total + rs[k]
    weight = total[24:25, :]
    mean = jnp.where(row < 24, total / jnp.where(weight > 0.0, weight, 1.0), 0.0)
    spread = spread_gain * (at - dot(gram, mean, HIGHEST))
    ag[i] = spread[: ag.shape[1]]
    copies = []
    for d in range(1, nx):
        copy = pltpu.make_async_remote_copy(
            src_ref=ag.at[i], dst_ref=ag.at[i],
            send_sem=send2.at[d], recv_sem=recv2.at[d],
            device_id=(lax.rem(i + d, nx), j), device_id_type=MESH,
        )
        copy.start()
        copies.append(copy)
    for copy in copies:
        copy.wait()
    out_ref[...] = ag[...]


def update_kernel(
    nx, info, spread_ref, meta_ref, wt_hi_hbm, wt_lo_hbm, base_hbm,
    out_hbm, moved, wt_hi, wt_lo, by_slot, sorted_s, num, weights, widen, sem,
):
    slots = spread_ref.shape[2]
    planes, tile_x, lanes = moved.shape
    base, count, group, blocks = block_tools(nx, lanes, info)
    load_h = pltpu.make_async_copy(wt_hi_hbm, wt_hi, sem.at[1])
    load_l = pltpu.make_async_copy(wt_lo_hbm, wt_lo, sem.at[2])
    load_s = pltpu.make_async_copy(base_hbm, moved, sem.at[0])
    load_h.start()
    load_l.start()
    load_s.start()

    def clear(b):
        where = pl.ds(pl.multiple_of(b * BLOCK, BLOCK), BLOCK)
        sorted_s[where, :] = jnp.full((BLOCK, lanes), -1.0, F32)

    for g in range(GROUPS):
        pl.when(count(g) > 0)(functools.partial(clear, base(g) + count(g) - 1))
    clear(blocks)
    wide = 3 * lanes
    for g in range(GROUPS):
        widen[g] = jnp.where(
            group_of(iota((lanes, wide), 1), g) == iota((lanes, wide), 0), 1.0, 0.0
        ).astype(BF16)
    num[...] = jnp.zeros(num.shape, F32)
    weights[...] = jnp.zeros(weights.shape, F32)

    pad = jnp.zeros((lanes - FEATURES, slots), F32)
    for k in range(nx):
        by_slot[k * slots : (k + 1) * slots, :] = jnp.concatenate(
            [spread_ref[k], meta_ref[k], pad], axis=0
        ).T

        def bring(n, carry):
            start = pl.multiple_of(n * 8, 8)
            got = by_slot[pl.ds(k * slots + start, 8), :]
            for m in range(8):
                sorted_s[pl.ds(info[2 * nx + k, start + m], 1), :] = got[m : m + 1, :]
            return carry

        lax.fori_loop(0, (info[3 * nx + k, 0] + 7) // 8, bring, 0)

    yy = iota((BLOCK, wide), 1) % 16
    load_h.wait()
    load_l.wait()

    def block_update(b):
        where = pl.ds(pl.multiple_of(b * BLOCK, BLOCK), BLOCK)
        g = group(b)
        value = sorted_s[where, :]
        y_here = value[:, 25:26].astype(I32)
        match = (value[:, 26:27] > 0.5) & (yy == y_here % 16)
        both = dot(jnp.concatenate(split(value), axis=0), widen[g])
        s_hi = jnp.where(match, both[:BLOCK], 0.0).astype(BF16)
        s_lo = jnp.where(match, both[BLOCK:], 0.0).astype(BF16)
        ones = jnp.where(match[:, :lanes], 1.0, 0.0).astype(BF16)
        w_hi, w_lo = wt_hi[:, where], wt_lo[:, where]
        right = jnp.concatenate([s_hi, ones], axis=1)
        added = dot(
            jnp.concatenate([w_hi, w_hi, w_lo], axis=1),
            jnp.concatenate(
                [right, jnp.concatenate([s_lo, jnp.zeros_like(ones)], axis=1), right], axis=0
            ),
        )
        return g, added

    def two_blocks(n, carry):
        for g, added in [block_update(2 * n), block_update(2 * n + 1)]:
            num[g] += added[:, :wide]
            weights[g] += added[:, wide:]
        return carry

    lax.fori_loop(0, (blocks + 1) // 2, two_blocks, 0)

    load_s.wait()
    chunk, parts = 8, 4
    length = tile_x // parts
    stores = []
    for part in range(parts):

        def finish(n, carry):
            here = pl.ds(pl.multiple_of(part * length + n * chunk, chunk), chunk)
            scale = [
                (time_step * nudge_gain) / jnp.maximum(weights[g, here, :], 1.0)
                for g in range(GROUPS)
            ]
            for v in range(3):
                gains = to_levels(
                    [num[g, here, v * lanes : (v + 1) * lanes] * scale[g] for g in range(GROUPS)]
                )
                for z in range(8):
                    moved[v * 8 + z, here, :] += gains[z]
            return carry

        lax.fori_loop(0, length // chunk, finish, 0)
        rows = pl.ds(part * length, length)
        stores.append(
            pltpu.make_async_copy(moved.at[:, rows, :], out_hbm.at[:, rows, :], sem.at[3 + part])
        )
        stores[-1].start()
    for copy in stores:
        copy.wait()


VM = pltpu.MemorySpace.VMEM


def vmem():
    return pl.BlockSpec(memory_space=VM)


def smem():
    return pl.BlockSpec(memory_space=pltpu.MemorySpace.SMEM)


def hbm():
    return pl.BlockSpec(memory_space=pl.ANY)


def gather_scratch(nx, slots, rows, cress_shape, grouped, lanes):
    across, tile_x = cress_shape
    return [
        pltpu.VMEM((tile_x // lanes, across, lanes), F32),
        pltpu.VMEM(grouped, BF16),
        pltpu.VMEM(grouped, BF16),
        pltpu.VMEM((tile_x // lanes, rows + 8, lanes), F32),
        pltpu.VMEM((rows + 8, lanes), I32),
        pltpu.VMEM((tile_x, rows), BF16),
        pltpu.VMEM((tile_x, rows), BF16),
        pltpu.VMEM((rows + 8, lanes), F32),
        pltpu.VMEM((nx * slots, lanes), F32),
        pltpu.VMEM((GROUPS, 3 * lanes, lanes), BF16),
        pltpu.SemaphoreType.DMA((7,)),
    ]


def update_scratch(nx, slots, rows, grouped, planes, lanes):
    tile_x = grouped[1]
    return [
        pltpu.VMEM((planes, tile_x, lanes), F32),
        pltpu.VMEM((tile_x, rows), BF16),
        pltpu.VMEM((tile_x, rows), BF16),
        pltpu.VMEM((nx * slots, lanes), F32),
        pltpu.VMEM((rows + 8, lanes), F32),
        pltpu.VMEM(grouped, F32),
        pltpu.VMEM((GROUPS, tile_x, lanes), F32),
        pltpu.VMEM((GROUPS, lanes, 3 * lanes), BF16),
        pltpu.SemaphoreType.DMA((7,)),
    ]


def local(nx, ny, model_state, obs_val, obs_owner, obs_x, obs_y, cressman, vertical):
    fields, levels, tile_x, lanes = model_state.shape
    planes = fields * levels
    recs = obs_val.shape[0]
    cap = max(2, 2 * recs // ny)
    slots = ny * cap
    rows = (slots * nx // BLOCK + GROUPS + 1) * BLOCK
    state = model_state.reshape(planes, tile_x, lanes)
    vert = vertical.reshape(planes, vertical.shape[2])
    shape = jax.ShapeDtypeStruct
    dma = pltpu.SemaphoreType.DMA
    limit = 56 * 1024 * 1024

    grouped = (GROUPS, tile_x, fields * lanes)
    at, info, meta, base, st_hi, st_lo = pl.pallas_call(
        functools.partial(dispatch_kernel, nx, ny),
        out_shape=(
            shape((FEATURES, slots), F32),
            shape((4 * nx + GROUPS, slots), I32),
            shape((nx, 8, slots), F32),
            shape((planes, tile_x, lanes), F32),
            shape(grouped, BF16),
            shape(grouped, BF16),
        ),
        in_specs=[vmem()] * 5 + [hbm()],
        out_specs=[vmem()] * 3 + [hbm()] * 3,
        scratch_shapes=[
            pltpu.VMEM((planes, tile_x + 16, lanes), F32),
            pltpu.VMEM((planes, tile_x, lanes), F32),
            pltpu.VMEM(grouped, BF16),
            pltpu.VMEM(grouped, BF16),
            pltpu.VMEM((slots, lanes), F32),
            pltpu.VMEM((slots, lanes), F32),
            pltpu.VMEM((nx, 8, slots), F32),
            pltpu.VMEM((3, nx, slots), F32),
            pltpu.VMEM((2, planes, lanes), F32),
            pltpu.VMEM((2 * planes, tile_x), F32),
            pltpu.VMEM((2, planes, lanes), F32),
            pltpu.VMEM((2, 2 * planes, tile_x), F32),
            dma,
            dma((3,)),
            dma((ny,)),
            dma((ny,)),
            dma((nx,)),
            dma((nx,)),
            dma((4,)),
            dma((4,)),
        ],
        compiler_params=pltpu.CompilerParams(
            collective_id=0, has_side_effects=True, vmem_limit_bytes=limit
        ),
        name="dispatch",
    )(
        obs_val, obs_owner.reshape(1, recs), obs_x.reshape(1, recs), obs_y.reshape(1, recs),
        vert, state,
    )

    part, wt_hi, wt_lo = pl.pallas_call(
        functools.partial(gather_kernel, nx),
        out_shape=(
            shape((nx, FEATURES, slots), F32),
            shape((tile_x, rows), BF16),
            shape((tile_x, rows), BF16),
        ),
        in_specs=[smem()] + [hbm()] * 3,
        out_specs=[vmem()] + [hbm()] * 2,
        scratch_shapes=gather_scratch(nx, slots, rows, cressman.shape, grouped, lanes),
        compiler_params=pltpu.CompilerParams(vmem_limit_bytes=limit),
        name="column_sums",
    )(info, cressman, st_hi, st_lo)

    spread = pl.pallas_call(
        functools.partial(reduce_kernel, nx),
        out_shape=shape((nx, planes, slots), F32),
        in_specs=[vmem()] * 3,
        out_specs=vmem(),
        scratch_shapes=[
            pltpu.VMEM((nx, FEATURES, slots), F32),
            pltpu.VMEM((nx, planes, slots), F32),
            dma((nx,)),
            dma((nx,)),
            dma((nx,)),
            dma((nx,)),
        ],
        compiler_params=pltpu.CompilerParams(
            collective_id=1, has_side_effects=True, vmem_limit_bytes=limit
        ),
        name="innovations",
    )(part, at, vert)

    out = pl.pallas_call(
        functools.partial(update_kernel, nx),
        out_shape=shape((planes, tile_x, lanes), F32),
        in_specs=[smem()] + [vmem()] * 2 + [hbm()] * 3,
        out_specs=hbm(),
        scratch_shapes=update_scratch(nx, slots, rows, grouped, planes, lanes),
        compiler_params=pltpu.CompilerParams(vmem_limit_bytes=limit),
        name="update",
    )(info, spread, meta, wt_hi, wt_lo, base)
    return out.reshape(model_state.shape)


def solution(mesh):
    in_specs = (
        P(None, None, "gx", "gy"),
        P(("gx", "gy"), None),
        P(("gx", "gy"), None),
        P(("gx", "gy")),
        P(("gx", "gy")),
        P(None, "gx"),
        P(),
    )
    out_specs = P(None, None, "gx", "gy")
    return jax.shard_map(
        functools.partial(local, mesh.shape["gx"], mesh.shape["gy"]),
        mesh=mesh, in_specs=in_specs, out_specs=out_specs, check_vma=False,
    )
```

time: 131 us -> 94.2 us (0.72)
  the two profiles are of different devices: /device:TPU:1 before, /device:TPU:33 now
where the time goes in v2:
time: 94.2 us; the launch traced here: 93.9 us
  Pallas kernels  93.9 us (100%)
    pallas_call x1, Pallas kernels, local(): pl.pallas_call(functools.partial(gather_kernel, nx), out_shape=(shape((nx...  30.9 us
    pallas_call x1, Pallas kernels, local(): pl.pallas_call(functools.partial(dispatch_kernel, nx, ny), out_shape=(sha...  23.7 us
    pallas_call x1, Pallas kernels, local(): pl.pallas_call(functools.partial(update_kernel, nx), out_shape=shape((pla...  23.2 us
    pallas_call x1, Pallas kernels, local(): pl.pallas_call(functools.partial(reduce_kernel, nx), out_shape=shape((nx,...  16.1 us

profile of v2, /device:TPU:33, one launch (start us, length us, event | category | flops | bytes accessed | tf_op | source)
XLA Modules:
  0.0 93.9 jit_solution(14371121592004502227)
XLA Ops:
  0.0 23.7 %dispatch.1 = (f32[32,256]{1,0:T(8,128)}, s32[40,256]{1,0:T(8,128)}, f32[8,8,256]{2,1,0:T(8,128)}, f32[24,384,128]{2,1,0:T(8,128)}, bf16[8,384,384]{2,1,0:T(8,128)(2,1)}, /*index=5*/bf16[8,384,384]{2,1,0:T(8,128)(2,1)}) custom-call(f32[128,384]{1,0:T(8,128)} %obs_ref.1, s32[1,128]{1,0:T(1,128)} %bitcast.9, s32[1,128]{1,0:T(1,128)} %bitcast.10, ...), custom_call_target="tpu_custom_call" | custom-call | tf_op jit(solution)/shard_map/dispatch/pallas_call | solution.py:643
  23.7 30.9 %column_sums.1 = (f32[8,32,256]{2,1,0:T(8,128)}, bf16[384,3200]{1,0:T(8,128)(2,1)}, bf16[384,3200]{1,0:T(8,128)(2,1)}) custom-call(s32[40,256]{1,0:T(8,128)} %get-tuple-element.14.info, f32[3072,384]{1,0:T(8,128)} %cress_hbm.1, bf16[8,384,384]{2,1,0:T(8,128)(2,1)} %get-tuple-element.15.high_hbm, bf16[8,384,384]{2,1,0:T(8,128)(2,1)} %get-tuple-element.16.low_hbm), custom_call_target="tpu_custom_call" | custom-call | tf_op jit(solution)/shard_map/column_sums/pallas_call | solution.py:686
  54.6 16.1 %innovations.1.spread_ref = f32[8,24,256]{2,1,0:T(8,128)} custom-call(f32[8,32,256]{2,1,0:T(8,128)} %get-tuple-element.17.part_ref, f32[32,256]{1,0:T(8,128)} %get-tuple-element.18.at_ref, f32[24,128]{1,0:T(8,128)} %bitcast.8), custom_call_target="tpu_custom_call" | custom-call | tf_op jit(solution)/shard_map/innovations/pallas_call | solution.py:700
  70.7 23.2 %update.1 = f32[24,384,128]{2,1,0:T(8,128)} custom-call(s32[40,256]{1,0:T(8,128)} %get-tuple-element.14.info, f32[8,24,256]{2,1,0:T(8,128)} %innovations.1.spread_ref, f32[8,8,256]{2,1,0:T(8,128)} %get-tuple-element.19.meta_ref, bf16[384,3200]{1,0:T(8,128)(2,1)} %get-tuple-element.20.wt_hi_hbm, bf16[384,3200]{1,0:T(8,128)(2,1)} %get-tuple-element.21.wt_lo_hbm, ...), custom_call_target="tpu_custom_call" | custom-call | tf_op jit(solution)/shard_map/update/pallas_call | solution.py:719

commit v3 on v2

--- a/solution.py
+++ b/solution.py
@@ -23,6 +23,8 @@
 FEATURES = 32
 GROUPS = 8
 BLOCK = 128
+CELLS = 4096
+STEP = 32
 
 
 def iota(shape, dim):
@@ -72,14 +74,13 @@
 
 def dispatch_kernel(
     nx, ny, obs_ref, owner_ref, x_ref, y_ref, vert_ref, state_hbm,
-    at_ref, info_ref, meta_ref, base_hbm, high_hbm, low_hbm,
-    plane, moved, st_hi, st_lo, sb, rb, mb, rows, xe, ye, xr, yr,
+    at_ref, info_ref, meta_ref, xh_ref, yh_ref, high_hbm, low_hbm,
+    plane, st_hi, st_lo, sb, rb, mb, rows, xe, ye, xr, yr,
     load_sem, store_sem, s1_send, s1_recv, s2_send, s2_recv, h_send, h_recv,
 ):
     i, j = lax.axis_index("gx"), lax.axis_index("gy")
-    planes, padded_x, lanes = plane.shape
-    tile_x = padded_x - 16
-    load = pltpu.make_async_copy(state_hbm, plane.at[:, 8 : 8 + tile_x, :], load_sem)
+    planes, tile_x, lanes = plane.shape
+    load = pltpu.make_async_copy(state_hbm, plane, load_sem)
     load.start()
     barrier = pltpu.get_barrier_semaphore()
     for d in range(1, ny):
@@ -132,12 +133,12 @@
 
     load.wait()
     for k in range(planes):
-        xe[0, k : k + 1, :] = plane[k, 7 + tile_x : 8 + tile_x, :]
-        xe[1, k : k + 1, :] = plane[k, 8:9, :]
+        xe[0, k : k + 1, :] = plane[k, tile_x - 1 : tile_x, :]
+        xe[1, k : k + 1, :] = plane[k, 0:1, :]
     edge_lane = iota((tile_x, lanes), 1)
 
     def gather_edges(k, edges):
-        turned = pltpu.roll(plane[k, 8 : 8 + tile_x, :], 2 * k + 1, 1)
+        turned = pltpu.roll(plane[k], 2 * k + 1, 1)
         return jnp.where(edge_lane // 2 == k, turned, edges)
 
     edges = lax.fori_loop(0, planes, gather_edges, jnp.zeros((tile_x, lanes), F32))
@@ -156,29 +157,6 @@
         copy.start()
         halo.append(copy)
 
-    chunk = 32
-
-    def group_chunk(n, carry):
-        start = pl.multiple_of(n * chunk, chunk)
-        here = pl.ds(start, chunk)
-        for v in range(3):
-            parts = to_groups(
-                [plane[v * 8 + z, pl.ds(pl.multiple_of(start + 8, 8), chunk), :] for z in range(8)]
-            )
-            for g in range(GROUPS):
-                high, low = split(parts[g])
-                st_hi[g, here, v * lanes : (v + 1) * lanes] = high
-                st_lo[g, here, v * lanes : (v + 1) * lanes] = low
-        return carry
-
-    lax.fori_loop(0, tile_x // chunk, group_chunk, 0)
-    stores = [
-        pltpu.make_async_copy(st_hi, high_hbm, store_sem.at[0]),
-        pltpu.make_async_copy(st_lo, low_hbm, store_sem.at[1]),
-    ]
-    for copy in stores:
-        copy.start()
-
     for copy in first:
         copy.wait()
     got = rb[...]
@@ -201,16 +179,232 @@
         )
         copy.start()
         second.append(copy)
+    chunk = 32
+
+    def group_chunk(n, carry):
+        here = pl.ds(pl.multiple_of(n * chunk, chunk), chunk)
+        for v in range(3):
+            parts = to_groups([plane[v * 8 + z, here, :] for z in range(8)])
+            for g in range(GROUPS):
+                high, low = split(parts[g])
+                st_hi[g, here, v * lanes : (v + 1) * lanes] = high
+                st_lo[g, here, v * lanes : (v + 1) * lanes] = low
+        return carry
+
+    lax.fori_loop(0, tile_x // chunk, group_chunk, 0)
+    stores = [
+        pltpu.make_async_copy(st_hi, high_hbm, store_sem.at[0]),
+        pltpu.make_async_copy(st_lo, low_hbm, store_sem.at[1]),
+    ]
+    for copy in stores:
+        copy.start()
+
     for copy in halo:
         copy.wait()
-    for k in range(planes):
-        plane[k, 7:8, :] = jnp.where(i > 0, xr[0, k : k + 1, :], 0.0)
-        plane[k, 8 + tile_x : 9 + tile_x, :] = jnp.where(i < nx - 1, xr[1, k : k + 1, :], 0.0)
+    xh_ref[0] = jnp.where(i > 0, xr[0], 0.0)
+    xh_ref[1] = jnp.where(i < nx - 1, xr[1], 0.0)
     even = iota((2 * planes, tile_x), 0) % 2 == 0
     south = jnp.where(j > 0, yr[0], 0.0)
     north = jnp.where(j < ny - 1, yr[1], 0.0)
+    yh_ref[...] = jnp.where(even, south, north)
+    for copy in second:
+        copy.wait()
+
+    for k in range(nx):
+        for f in range(3):
+            rows[f, k : k + 1, :] = mb[k, f : f + 1, :]
+    y_cells = rows[1].astype(I32)
+    valid = rows[2] > 0.5
+    group = jnp.where(valid, y_cells // (lanes // GROUPS), GROUPS)
+    masks = jnp.concatenate(
+        [jnp.where(group == g, 1.0, 0.0) for g in range(GROUPS)], axis=0
+    )
+    lines = GROUPS * nx
+    after = jnp.where(iota((slots, slots), 0) < iota((slots, slots), 1), 1.0, 0.0)
+    rank = dot(masks, after)
+    total = jnp.broadcast_to(jnp.sum(masks, axis=1, keepdims=True), (lines, lanes))
+    line, other = iota((lines, lines), 0), iota((lines, lines), 1)
+    same = line // nx == other // nx
+    offset = dot(jnp.where(same & (other < line), 1.0, 0.0), total, HIGHEST)
+    whole = dot(jnp.where(same, 1.0, 0.0), total, HIGHEST)
+    count = (whole.astype(I32) + (BLOCK - 1)) // BLOCK
+    base = dot(
+        jnp.where((other // nx < line // nx) & (other % nx == 0), 1.0, 0.0),
+        count.astype(F32),
+        HIGHEST,
+    )
+    placed = masks * (base[:, 0:1] * BLOCK + offset[:, 0:1] + rank)
+    pos = placed[0:nx]
+    for g in range(1, GROUPS):
+        pos = pos + placed[g * nx : (g + 1) * nx]
+    dump = (slots * nx // BLOCK + GROUPS + 1) * BLOCK
+    place = jnp.where(valid, pos.astype(I32), dump)
+    info_ref[0:nx, :] = (
+        place + (rows[0].astype(I32) + y_cells % (lanes // GROUPS) * CELLS) * CELLS
+    )
+    info_ref[nx : 2 * nx, :] = jnp.broadcast_to(
+        jnp.sum(rows[2], axis=1, keepdims=True), (nx, slots)
+    ).astype(I32)
+    base = base.astype(I32)
+    for g in range(GROUPS):
+        info_ref[2 * nx + g : 2 * nx + g + 1, 0:lanes] = base[g * nx : g * nx + 1, :]
+        info_ref[2 * nx + g : 2 * nx + g + 1, lanes : 2 * lanes] = count[g * nx : g * nx + 1, :]
+    meta_ref[...] = mb[...]
+    for copy in stores:
+        copy.wait()
+
+
+def block_tools(nx, lanes, info):
+    def base(g):
+        return info[2 * nx + g, 0]
+
+    def count(g):
+        return info[2 * nx + g, lanes]
+
+    def group(b):
+        found = 0
+        for g in range(1, GROUPS):
+            found = found + jnp.where(b >= base(g), 1, 0)
+        return found
+
+    return base, count, group, base(GROUPS - 1) + count(GROUPS - 1)
+
+
+def gather_kernel(
+    nx, info, cress_hbm, high_hbm, low_hbm, part_ref, wt_hi_hbm, wt_lo_hbm,
+    cress, st_hi, st_lo, sorted_w, chosen, totals, wt_hi, wt_lo, sums, by_slot, fold, sem,
+):
+    slots = info.shape[1]
+    lanes = cress.shape[2]
+    tile_x = cress_hbm.shape[1]
+    pieces = tile_x // lanes
+    rows = wt_hi.shape[1]
+    base, count, group, blocks = block_tools(nx, lanes, info)
+    loads = [
+        pltpu.make_async_copy(
+            cress_hbm.at[:, c * lanes : (c + 1) * lanes], cress.at[:, c, :], sem.at[c]
+        )
+        for c in range(pieces)
+    ]
+    state_loads = [
+        pltpu.make_async_copy(high_hbm, st_hi, sem.at[3]),
+        pltpu.make_async_copy(low_hbm, st_lo, sem.at[4]),
+    ]
+    for copy in loads + state_loads:
+        copy.start()
+    y_line = iota((8, lanes), 0) == pieces
+    blank = jnp.where(y_line, -1.0, jnp.zeros((8, lanes), F32))
+
+    def clear(b):
+        where = pl.ds(pl.multiple_of(b * BLOCK, BLOCK), BLOCK)
+        sorted_w[where] = jnp.broadcast_to(blank[None], (BLOCK, 8, lanes))
+
+    for g in range(GROUPS):
+        pl.when(count(g) > 0)(functools.partial(clear, base(g) + count(g) - 1))
+    clear(blocks)
+    wide = 3 * lanes
+    for g in range(GROUPS):
+        fold[g] = jnp.where(
+            group_of(iota((wide, lanes), 0), g) == iota((wide, lanes), 1), 1.0, 0.0
+        ).astype(BF16)
+
+    for copy in loads:
+        copy.wait()
+    for k in range(nx):
+
+        def bring(n, carry):
+            entries = [info[k, n * STEP + m] for m in range(STEP)]
+            got = [
+                jnp.where(y_line, (lax.shift_right_logical(e, 24)).astype(F32), cress[lax.shift_right_logical(e, 12) & (CELLS - 1)])
+                for e in entries
+            ]
+            for e, row in zip(entries, got):
+                sorted_w[e & (CELLS - 1)] = row
+            return carry
+
+        lax.fori_loop(0, (info[nx + k, 0] + STEP - 1) // STEP, bring, 0)
+
+    for copy in state_loads:
+        copy.wait()
+    yy = (iota((BLOCK, wide), 1) % 16).astype(F32)
+    lane = iota((BLOCK, lanes), 1)
+
+    def multiply(b):
+        b = jnp.minimum(b, blocks)
+        where = pl.ds(pl.multiple_of(b * BLOCK, BLOCK), BLOCK)
+        g = group(b)
+        parts = [sorted_w[where, c, :] for c in range(pieces)]
+        high, low = split(jnp.concatenate(parts, axis=1))
+        both = dot(jnp.concatenate([high, low], axis=0), st_hi[g])
+        products = both[:BLOCK] + both[BLOCK:] + dot(high, st_lo[g])
+        y_here = sorted_w[where, pieces, :]
+        y_wide = jnp.concatenate([y_here, y_here, y_here], axis=1)
+        high, low = split(jnp.where(yy == y_wide, products, 0.0))
+        total = jnp.sum(parts[0] + parts[1] + parts[2], axis=1, keepdims=True)
+        return where, high, low, total, [split(part.T) for part in parts]
+
+    def two_blocks(n, carry):
+        for m in range(2):
+            b = 2 * n - 2 + m
+            both = dot(chosen[m], fold[group(b)])
+            result = jnp.where(lane == 24, totals[m], both[:BLOCK] + both[BLOCK:])
+            start = jnp.where(b < 0, rows + m * BLOCK, b * BLOCK)
+            sums[pl.ds(pl.multiple_of(start, BLOCK), BLOCK), :] = result
+        for m, (where, high, low, total, turned) in enumerate(
+            [multiply(2 * n), multiply(2 * n + 1)]
+        ):
+            chosen[m, :BLOCK, :] = high
+            chosen[m, BLOCK:, :] = low
+            totals[m] = jnp.broadcast_to(total, (BLOCK, lanes))
+            for c in range(pieces):
+                wt_hi[c * lanes : (c + 1) * lanes, where] = turned[c][0]
+                wt_lo[c * lanes : (c + 1) * lanes, where] = turned[c][1]
+        return carry
+
+    lax.fori_loop(0, (blocks + 1) // 2 + 1, two_blocks, 0)
+    stores = [
+        pltpu.make_async_copy(wt_hi, wt_hi_hbm, sem.at[5]),
+        pltpu.make_async_copy(wt_lo, wt_lo_hbm, sem.at[6]),
+    ]
+    for copy in stores:
+        copy.start()
+
+    by_slot[...] = jnp.zeros(by_slot.shape, F32)
+    for k in range(nx):
+
+        def give(n, carry):
+            start = pl.multiple_of(k * slots + n * STEP, STEP)
+            entries = [info[k, n * STEP + m] for m in range(STEP)]
+            got = [sums[pl.ds(e & (CELLS - 1), 1), :] for e in entries]
+            for m in range(STEP):
+                by_slot[pl.ds(start + m, 1), :] = got[m]
+            return carry
+
+        lax.fori_loop(0, (info[nx + k, 0] + STEP - 1) // STEP, give, 0)
+        part_ref[k] = by_slot[k * slots : (k + 1) * slots, :].T[:FEATURES]
+    for copy in stores:
+        copy.wait()
+
+
+def reduce_kernel(
+    nx, part_ref, at_ref, vert_ref, xh_ref, yh_ref, state_hbm, out_ref, base_hbm,
+    plane, moved, rs, ag, load_sem, store_sem, send1, recv1, send2, recv2,
+):
+    i, j = lax.axis_index("gx"), lax.axis_index("gy")
+    planes, padded_x, lanes = plane.shape
+    tile_x = padded_x - 16
+    load = pltpu.make_async_copy(state_hbm, plane.at[:, 8 : 8 + tile_x, :], load_sem)
+    load.start()
+    barrier = pltpu.get_barrier_semaphore()
+    for d in range(1, nx):
+        pl.semaphore_signal(
+            barrier, inc=1, device_id=(lax.rem(i + d, nx), j), device_id_type=MESH
+        )
+    for k in range(planes):
+        plane[k, 7:8, :] = xh_ref[0, k : k + 1, :]
+        plane[k, 8 + tile_x : 9 + tile_x, :] = xh_ref[1, k : k + 1, :]
     beside = jnp.concatenate(
-        [jnp.where(even, south, north), jnp.zeros((lanes - 2 * planes, tile_x), F32)], axis=0
+        [yh_ref[...], jnp.zeros((lanes - 2 * planes, tile_x), F32)], axis=0
     ).T
     beside_high, beside_low = split(beside)
     beside = jnp.where(
@@ -252,186 +446,12 @@
         )
         return carry
 
-    lax.fori_loop(0, planes, move, 0)
-    stores.append(pltpu.make_async_copy(moved, base_hbm, store_sem.at[2]))
-    stores[2].start()
-    for copy in second:
-        copy.wait()
-
-    for k in range(nx):
-        for f in range(3):
-            rows[f, k : k + 1, :] = mb[k, f : f + 1, :]
-    y_cells = rows[1].astype(I32)
-    valid = rows[2] > 0.5
-    group = jnp.where(valid, y_cells // (lanes // GROUPS), GROUPS)
-    masks = jnp.concatenate(
-        [jnp.where(group == g, 1.0, 0.0) for g in range(GROUPS)], axis=0
-    )
-    lines = GROUPS * nx
-    after = jnp.where(iota((slots, slots), 0) < iota((slots, slots), 1), 1.0, 0.0)
-    rank = dot(masks, after)
-    total = jnp.broadcast_to(jnp.sum(masks, axis=1, keepdims=True), (lines, lanes))
-    line, other = iota((lines, lines), 0), iota((lines, lines), 1)
-    same = line // nx == other // nx
-    offset = dot(jnp.where(same & (other < line), 1.0, 0.0), total, HIGHEST)
-    whole = dot(jnp.where(same, 1.0, 0.0), total, HIGHEST)
-    count = (whole.astype(I32) + (BLOCK - 1)) // BLOCK
-    base = dot(
-        jnp.where((other // nx < line // nx) & (other % nx == 0), 1.0, 0.0),
-        count.astype(F32),
-        HIGHEST,
-    )
-    placed = masks * (base[:, 0:1] * BLOCK + offset[:, 0:1] + rank)
-    pos = placed[0:nx]
-    for g in range(1, GROUPS):
-        pos = pos + placed[g * nx : (g + 1) * nx]
-    dump = (slots * nx // BLOCK + GROUPS + 1) * BLOCK
-    info_ref[0:nx, :] = rows[0].astype(I32)
-    info_ref[nx : 2 * nx, :] = y_cells % (lanes // GROUPS)
-    info_ref[2 * nx : 3 * nx, :] = jnp.where(valid, pos.astype(I32), dump)
-    info_ref[3 * nx : 4 * nx, :] = jnp.broadcast_to(
-        jnp.sum(rows[2], axis=1, keepdims=True), (nx, slots)
-    ).astype(I32)
-    base = base.astype(I32)
-    for g in range(GROUPS):
-        info_ref[4 * nx + g : 4 * nx + g + 1, 0:lanes] = base[g * nx : g * nx + 1, :]
-        info_ref[4 * nx + g : 4 * nx + g + 1, lanes : 2 * lanes] = count[g * nx : g * nx + 1, :]
-    meta_ref[...] = mb[...]
-    for copy in stores:
-        copy.wait()
-
-
-def block_tools(nx, lanes, info):
-    def base(g):
-        return info[4 * nx + g, 0]
-
-    def count(g):
-        return info[4 * nx + g, lanes]
-
-    def group(b):
-        found = 0
-        for g in range(1, GROUPS):
-            found = found + jnp.where(b >= base(g), 1, 0)
-        return found
-
-    return base, count, group, base(GROUPS - 1) + count(GROUPS - 1)
-
-
-def gather_kernel(
-    nx, info, cress_hbm, high_hbm, low_hbm, part_ref, wt_hi_hbm, wt_lo_hbm,
-    cress, st_hi, st_lo, sorted_w, sorted_y, wt_hi, wt_lo, sums, by_slot, fold, sem,
-):
-    slots = info.shape[1]
-    pieces, _, lanes = cress.shape
-    tile_x = pieces * lanes
-    base, count, group, blocks = block_tools(nx, lanes, info)
-    loads = [
-        pltpu.make_async_copy(
-            cress_hbm.at[:, c * lanes : (c + 1) * lanes], cress.at[c], sem.at[c]
-        )
-        for c in range(pieces)
-    ]
-    state_loads = [
-        pltpu.make_async_copy(high_hbm, st_hi, sem.at[3]),
-        pltpu.make_async_copy(low_hbm, st_lo, sem.at[4]),
-    ]
-    for copy in loads + state_loads:
-        copy.start()
-
-    def clear(b):
-        where = pl.ds(pl.multiple_of(b * BLOCK, BLOCK), BLOCK)
-        for c in range(pieces):
-            sorted_w[c, where, :] = jnp.zeros((BLOCK, lanes), F32)
-        sorted_y[where, :] = jnp.full((BLOCK, lanes), -1, I32)
-
-    for g in range(GROUPS):
-        pl.when(count(g) > 0)(functools.partial(clear, base(g) + count(g) - 1))
-    clear(blocks)
-    wide = 3 * lanes
-    for g in range(GROUPS):
-        fold[g] = jnp.where(
-            group_of(iota((wide, lanes), 0), g) == iota((wide, lanes), 1), 1.0, 0.0
-        ).astype(BF16)
-
-    for copy in loads:
-        copy.wait()
-    for k in range(nx):
-
-        def bring(n, carry):
-            at = [n * 8 + m for m in range(8)]
-            cells = [info[k, s] for s in at]
-            places = [info[2 * nx + k, s] for s in at]
-            got = [[cress[c, pl.ds(x, 1), :] for c in range(pieces)] for x in cells]
-            for p, found in zip(places, got):
-                for c in range(pieces):
-                    sorted_w[c, pl.ds(p, 1), :] = found[c]
-            for p, s in zip(places, at):
-                sorted_y[pl.ds(p, 1), :] = jnp.full((1, lanes), info[nx + k, s], I32)
-            return carry
-
-        lax.fori_loop(0, (info[3 * nx + k, 0] + 7) // 8, bring, 0)
-
-    for copy in state_loads:
-        copy.wait()
-    yy = iota((BLOCK, wide), 1) % 16
-    lane = iota((BLOCK, lanes), 1)
-
-    def block_sums(b):
-        where = pl.ds(pl.multiple_of(b * BLOCK, BLOCK), BLOCK)
-        g = group(b)
-        parts = [sorted_w[c, where, :] for c in range(pieces)]
-        high, low = split(jnp.concatenate(parts, axis=1))
-        both = dot(jnp.concatenate([high, low], axis=0), st_hi[g])
-        products = both[:BLOCK] + both[BLOCK:] + dot(high, st_lo[g])
-        y_here = sorted_y[where, :]
-        y_wide = jnp.concatenate([y_here, y_here, y_here], axis=1)
-        chosen = split(jnp.where(yy == y_wide, products, 0.0))
-        both = dot(jnp.concatenate(chosen, axis=0), fold[g])
-        total = jnp.sum(parts[0] + parts[1] + parts[2], axis=1, keepdims=True)
-        result = jnp.where(lane == 24, total, both[:BLOCK] + both[BLOCK:])
-        turned = [split(part.T) for part in parts]
-        return where, result, turned
-
-    def two_blocks(n, carry):
-        for where, result, turned in [block_sums(2 * n), block_sums(2 * n + 1)]:
-            sums[where, :] = result
-            for c in range(pieces):
-                wt_hi[c * lanes : (c + 1) * lanes, where] = turned[c][0]
-                wt_lo[c * lanes : (c + 1) * lanes, where] = turned[c][1]
-        return carry
-
-    lax.fori_loop(0, (blocks + 1) // 2, two_blocks, 0)
-    stores = [
-        pltpu.make_async_copy(wt_hi, wt_hi_hbm, sem.at[5]),
-        pltpu.make_async_copy(wt_lo, wt_lo_hbm, sem.at[6]),
-    ]
-    for copy in stores:
-        copy.start()
-
-    by_slot[...] = jnp.zeros(by_slot.shape, F32)
-    for k in range(nx):
-
-        def give(n, carry):
-            start = pl.multiple_of(n * 8, 8)
-            got = [sums[pl.ds(info[2 * nx + k, start + m], 1), :] for m in range(8)]
-            by_slot[pl.ds(k * slots + start, 8), :] = jnp.concatenate(got, axis=0)
-            return carry
-
-        lax.fori_loop(0, (info[3 * nx + k, 0] + 7) // 8, give, 0)
-        part_ref[k] = by_slot[k * slots : (k + 1) * slots, :].T[:FEATURES]
-    for copy in stores:
-        copy.wait()
-
-
-def reduce_kernel(
-    nx, part_ref, at_ref, vert_ref, out_ref, rs, ag, send1, recv1, send2, recv2
-):
-    i, j = lax.axis_index("gx"), lax.axis_index("gy")
-    barrier = pltpu.get_barrier_semaphore()
-    for d in range(1, nx):
-        pl.semaphore_signal(
-            barrier, inc=1, device_id=(lax.rem(i + d, nx), j), device_id_type=MESH
-        )
+    vert = jnp.concatenate([vert_ref[...], jnp.zeros((8, lanes), F32)], axis=0)
+    same = iota((FEATURES, FEATURES), 0) // 8 == iota((FEATURES, FEATURES), 1) // 8
+    gram = jnp.where(same, dot_t(vert, vert, HIGHEST), 0.0)
+    at = at_ref[...]
+    row = iota(at.shape, 0)
+
     pl.semaphore_wait(barrier, nx - 1)
     copies = []
     for d in range(1, nx):
@@ -444,12 +464,11 @@
         copy.start()
         copies.append(copy)
     rs[i] = part_ref[i]
-    lanes = vert_ref.shape[1]
-    vert = jnp.concatenate([vert_ref[...], jnp.zeros((8, lanes), F32)], axis=0)
-    same = iota((FEATURES, FEATURES), 0) // 8 == iota((FEATURES, FEATURES), 1) // 8
-    gram = jnp.where(same, dot_t(vert, vert, HIGHEST), 0.0)
-    at = at_ref[...]
-    row = iota(at.shape, 0)
+    load.wait()
+    half = planes // 2
+    lax.fori_loop(0, half, move, 0)
+    stores = [pltpu.make_async_copy(moved.at[0:half], base_hbm.at[0:half], store_sem.at[0])]
+    stores[0].start()
     for copy in copies:
         copy.wait()
     total = rs[0]
@@ -468,14 +487,21 @@
         )
         copy.start()
         copies.append(copy)
+    lax.fori_loop(half, planes, move, 0)
+    stores.append(
+        pltpu.make_async_copy(moved.at[half:planes], base_hbm.at[half:planes], store_sem.at[1])
+    )
+    stores[1].start()
     for copy in copies:
         copy.wait()
     out_ref[...] = ag[...]
+    for copy in stores:
+        copy.wait()
 
 
 def update_kernel(
     nx, info, spread_ref, meta_ref, wt_hi_hbm, wt_lo_hbm, base_hbm,
-    out_hbm, moved, wt_hi, wt_lo, by_slot, sorted_s, num, weights, widen, sem,
+    out_hbm, moved, wt_hi, wt_lo, by_slot, sorted_s, right, num, weights, widen, sem,
 ):
     slots = spread_ref.shape[2]
     planes, tile_x, lanes = moved.shape
@@ -509,45 +535,51 @@
         ).T
 
         def bring(n, carry):
-            start = pl.multiple_of(n * 8, 8)
-            got = by_slot[pl.ds(k * slots + start, 8), :]
-            for m in range(8):
-                sorted_s[pl.ds(info[2 * nx + k, start + m], 1), :] = got[m : m + 1, :]
+            start = pl.multiple_of(k * slots + n * STEP, STEP)
+            entries = [info[k, n * STEP + m] for m in range(STEP)]
+            got = [by_slot[pl.ds(start + m, 1), :] for m in range(STEP)]
+            for e, row in zip(entries, got):
+                sorted_s[pl.ds(e & (CELLS - 1), 1), :] = row
             return carry
 
-        lax.fori_loop(0, (info[3 * nx + k, 0] + 7) // 8, bring, 0)
+        lax.fori_loop(0, (info[nx + k, 0] + STEP - 1) // STEP, bring, 0)
 
     yy = iota((BLOCK, wide), 1) % 16
     load_h.wait()
     load_l.wait()
 
-    def block_update(b):
-        where = pl.ds(pl.multiple_of(b * BLOCK, BLOCK), BLOCK)
-        g = group(b)
+    right[...] = jnp.zeros(right.shape, BF16)
+
+    def widened(b):
+        where = pl.ds(pl.multiple_of(jnp.minimum(b, blocks) * BLOCK, BLOCK), BLOCK)
         value = sorted_s[where, :]
         y_here = value[:, 25:26].astype(I32)
         match = (value[:, 26:27] > 0.5) & (yy == y_here % 16)
-        both = dot(jnp.concatenate(split(value), axis=0), widen[g])
+        both = dot(jnp.concatenate(split(value), axis=0), widen[group(b)])
         s_hi = jnp.where(match, both[:BLOCK], 0.0).astype(BF16)
         s_lo = jnp.where(match, both[BLOCK:], 0.0).astype(BF16)
         ones = jnp.where(match[:, :lanes], 1.0, 0.0).astype(BF16)
+        return s_hi, s_lo, ones
+
+    def block_update(b, m):
+        where = pl.ds(pl.multiple_of(jnp.maximum(b, 0) * BLOCK, BLOCK), BLOCK)
         w_hi, w_lo = wt_hi[:, where], wt_lo[:, where]
-        right = jnp.concatenate([s_hi, ones], axis=1)
-        added = dot(
-            jnp.concatenate([w_hi, w_hi, w_lo], axis=1),
-            jnp.concatenate(
-                [right, jnp.concatenate([s_lo, jnp.zeros_like(ones)], axis=1), right], axis=0
-            ),
-        )
-        return g, added
+        return group(b), dot(jnp.concatenate([w_hi, w_hi, w_lo], axis=1), right[m])
 
     def two_blocks(n, carry):
-        for g, added in [block_update(2 * n), block_update(2 * n + 1)]:
+        results = [block_update(2 * n - 2 + m, m) for m in range(2)]
+        for m, (s_hi, s_lo, ones) in enumerate([widened(2 * n), widened(2 * n + 1)]):
+            right[m, 0:BLOCK, :wide] = s_hi
+            right[m, BLOCK : 2 * BLOCK, :wide] = s_lo
+            right[m, 2 * BLOCK : 3 * BLOCK, :wide] = s_hi
+            right[m, 0:BLOCK, wide:] = ones
+            right[m, 2 * BLOCK : 3 * BLOCK, wide:] = ones
+        for g, added in results:
             num[g] += added[:, :wide]
             weights[g] += added[:, wide:]
         return carry
 
-    lax.fori_loop(0, (blocks + 1) // 2, two_blocks, 0)
+    lax.fori_loop(0, (blocks + 1) // 2 + 1, two_blocks, 0)
 
     load_s.wait()
     chunk, parts = 8, 4
@@ -597,14 +629,15 @@
 def gather_scratch(nx, slots, rows, cress_shape, grouped, lanes):
     across, tile_x = cress_shape
     return [
-        pltpu.VMEM((tile_x // lanes, across, lanes), F32),
+        pltpu.VMEM((across, 8, lanes), F32),
         pltpu.VMEM(grouped, BF16),
         pltpu.VMEM(grouped, BF16),
-        pltpu.VMEM((tile_x // lanes, rows + 8, lanes), F32),
-        pltpu.VMEM((rows + 8, lanes), I32),
+        pltpu.VMEM((rows + 8, 8, lanes), F32),
+        pltpu.VMEM((2, 2 * BLOCK, 3 * lanes), BF16),
+        pltpu.VMEM((2, BLOCK, lanes), F32),
         pltpu.VMEM((tile_x, rows), BF16),
         pltpu.VMEM((tile_x, rows), BF16),
-        pltpu.VMEM((rows + 8, lanes), F32),
+        pltpu.VMEM((rows + 2 * BLOCK, lanes), F32),
         pltpu.VMEM((nx * slots, lanes), F32),
         pltpu.VMEM((GROUPS, 3 * lanes, lanes), BF16),
         pltpu.SemaphoreType.DMA((7,)),
@@ -619,6 +652,7 @@
         pltpu.VMEM((tile_x, rows), BF16),
         pltpu.VMEM((nx * slots, lanes), F32),
         pltpu.VMEM((rows + 8, lanes), F32),
+        pltpu.VMEM((2, 3 * BLOCK, 4 * lanes), BF16),
         pltpu.VMEM(grouped, F32),
         pltpu.VMEM((GROUPS, tile_x, lanes), F32),
         pltpu.VMEM((GROUPS, lanes, 3 * lanes), BF16),
@@ -640,20 +674,20 @@
     limit = 56 * 1024 * 1024
 
     grouped = (GROUPS, tile_x, fields * lanes)
-    at, info, meta, base, st_hi, st_lo = pl.pallas_call(
+    at, info, meta, xh, yh, st_hi, st_lo = pl.pallas_call(
         functools.partial(dispatch_kernel, nx, ny),
         out_shape=(
             shape((FEATURES, slots), F32),
-            shape((4 * nx + GROUPS, slots), I32),
+            shape((2 * nx + GROUPS, slots), I32),
             shape((nx, 8, slots), F32),
-            shape((planes, tile_x, lanes), F32),
+            shape((2, planes, lanes), F32),
+            shape((2 * planes, tile_x), F32),
             shape(grouped, BF16),
             shape(grouped, BF16),
         ),
         in_specs=[vmem()] * 5 + [hbm()],
-        out_specs=[vmem()] * 3 + [hbm()] * 3,
+        out_specs=[vmem()] * 5 + [hbm()] * 2,
         scratch_shapes=[
-            pltpu.VMEM((planes, tile_x + 16, lanes), F32),
             pltpu.VMEM((planes, tile_x, lanes), F32),
             pltpu.VMEM(grouped, BF16),
             pltpu.VMEM(grouped, BF16),
@@ -666,7 +700,7 @@
             pltpu.VMEM((2, planes, lanes), F32),
             pltpu.VMEM((2, 2 * planes, tile_x), F32),
             dma,
-            dma((3,)),
+            dma((2,)),
             dma((ny,)),
             dma((ny,)),
             dma((nx,)),
@@ -697,14 +731,18 @@
         name="column_sums",
     )(info, cressman, st_hi, st_lo)
 
-    spread = pl.pallas_call(
+    spread, base = pl.pallas_call(
         functools.partial(reduce_kernel, nx),
-        out_shape=shape((nx, planes, slots), F32),
-        in_specs=[vmem()] * 3,
-        out_specs=vmem(),
+        out_shape=(shape((nx, planes, slots), F32), shape((planes, tile_x, lanes), F32)),
+        in_specs=[vmem()] * 5 + [hbm()],
+        out_specs=[vmem(), hbm()],
         scratch_shapes=[
+            pltpu.VMEM((planes, tile_x + 16, lanes), F32),
+            pltpu.VMEM((planes, tile_x, lanes), F32),
             pltpu.VMEM((nx, FEATURES, slots), F32),
             pltpu.VMEM((nx, planes, slots), F32),
+            dma,
+            dma((2,)),
             dma((nx,)),
             dma((nx,)),
             dma((nx,)),
@@ -714,7 +752,7 @@
             collective_id=1, has_side_effects=True, vmem_limit_bytes=limit
         ),
         name="innovations",
-    )(part, at, vert)
+    )(part, at, vert, xh, yh, state)
 
     out = pl.pallas_call(
         functools.partial(update_kernel, nx),

time: 94.2 us -> 81.7 us (0.87)
  the two profiles are of different devices: /device:TPU:33 before, /device:TPU:35 now
where the time goes in v3:
time: 81.7 us; the launch traced here: 81.4 us
  Pallas kernels  81.4 us (100%)
    pallas_call x1, Pallas kernels, local(): pl.pallas_call(functools.partial(gather_kernel, nx), out_shape=(shape((nx...  28.7 us
    pallas_call x1, Pallas kernels, local(): pl.pallas_call(functools.partial(update_kernel, nx), out_shape=shape((pla...  21.2 us
    pallas_call x1, Pallas kernels, local(): pl.pallas_call(functools.partial(dispatch_kernel, nx, ny), out_shape=(sha...  17.2 us
    pallas_call x1, Pallas kernels, local(): pl.pallas_call(functools.partial(reduce_kernel, nx), out_shape=(shape((nx...  14.3 us

profile of v3, /device:TPU:35, one launch (start us, length us, event | category | flops | bytes accessed | tf_op | source)
XLA Modules:
  0.0 81.4 jit_solution(10362582414388133744)
XLA Ops:
  0.0 17.2 %dispatch.1 = (f32[32,256]{1,0:T(8,128)}, s32[24,256]{1,0:T(8,128)}, f32[8,8,256]{2,1,0:T(8,128)}, f32[2,24,128]{2,1,0:T(8,128)}, f32[48,384]{1,0:T(8,128)}, /*i...) custom-call(f32[128,384]{1,0:T(8,128)} %obs_ref.1, s32[1,128]{1,0:T(1,128)} %bitcast.10, s32[1,128]{1,0:T(1,128)} %bitcast.11, ...), custom_call_target="tpu_custom_call" | custom-call | tf_op jit(solution)/shard_map/dispatch/pallas_call | solution.py:677
  17.2 28.7 %column_sums.1 = (f32[8,32,256]{2,1,0:T(8,128)}, bf16[384,3200]{1,0:T(8,128)(2,1)}, bf16[384,3200]{1,0:T(8,128)(2,1)}) custom-call(s32[24,256]{1,0:T(8,128)} %get-tuple-element.17.info, f32[3072,384]{1,0:T(8,128)} %cress_hbm.1, bf16[8,384,384]{2,1,0:T(8,128)(2,1)} %get-tuple-element.18.high_hbm, bf16[8,384,384]{2,1,0:T(8,128)(2,1)} %get-tuple-element.19.low_hbm), custom_call_target="tpu_custom_call" | custom-call | tf_op jit(solution)/shard_map/column_sums/pallas_call | solution.py:720
  46.0 14.3 %innovations.1 = (f32[8,24,256]{2,1,0:T(8,128)}, f32[24,384,128]{2,1,0:T(8,128)}) custom-call(f32[8,32,256]{2,1,0:T(8,128)} %get-tuple-element.20.part_ref, f32[32,256]{1,0:T(8,128)} %get-tuple-element.21.at_ref, f32[24,128]{1,0:T(8,128)} %bitcast.9, f32[2,24,128]{2,1,0:T(8,128)} %get-tuple-element.22.xh_ref, f32[48,384]{1,0:T(8,128)} %get-tuple-element.23.yh_ref, ...), custom_call_target="tpu_custom_call" | custom-call | tf_op jit(solution)/shard_map/innovations/pallas_call | solution.py:734
  60.2 21.2 %update.1 = f32[24,384,128]{2,1,0:T(8,128)} custom-call(s32[24,256]{1,0:T(8,128)} %get-tuple-element.17.info, f32[8,24,256]{2,1,0:T(8,128)} %get-tuple-element.24.spread_ref, f32[8,8,256]{2,1,0:T(8,128)} %get-tuple-element.25.meta_ref, bf16[384,3200]{1,0:T(8,128)(2,1)} %get-tuple-element.26.wt_hi_hbm, bf16[384,3200]{1,0:T(8,128)(2,1)} %get-tuple-element.27.wt_lo_hbm, ...), custom_call_target="tpu_custom_call" | custom-call | tf_op jit(solution)/shard_map/update/pallas_call | solution.py:757

commit v4 on v3

--- a/solution.py
+++ b/solution.py
@@ -74,7 +74,7 @@
 
 def dispatch_kernel(
     nx, ny, obs_ref, owner_ref, x_ref, y_ref, vert_ref, state_hbm,
-    at_ref, info_ref, meta_ref, xh_ref, yh_ref, high_hbm, low_hbm,
+    info_ref, meta_ref, xh_ref, yh_ref, high_hbm, low_hbm,
     plane, st_hi, st_lo, sb, rb, mb, rows, xe, ye, xr, yr,
     load_sem, store_sem, s1_send, s1_recv, s2_send, s2_recv, h_send, h_recv,
 ):
@@ -167,9 +167,7 @@
     place = jnp.where(
         (iota((slots, slots), 1) == rank.astype(I32)) & (valid > 0.5), 1.0, 0.0
     )
-    compact = dot(got_t, place, HIGHEST)
-    at_ref[...] = compact
-    mb[i] = compact[24:32]
+    mb[i] = dot(got_t, place, HIGHEST)
     second = []
     for d in range(1, nx):
         copy = pltpu.make_async_remote_copy(
@@ -212,7 +210,7 @@
 
     for k in range(nx):
         for f in range(3):
-            rows[f, k : k + 1, :] = mb[k, f : f + 1, :]
+            rows[f, k : k + 1, :] = mb[k, 24 + f : 25 + f, :]
     y_cells = rows[1].astype(I32)
     valid = rows[2] > 0.5
     group = jnp.where(valid, y_cells // (lanes // GROUPS), GROUPS)
@@ -237,11 +235,8 @@
     pos = placed[0:nx]
     for g in range(1, GROUPS):
         pos = pos + placed[g * nx : (g + 1) * nx]
-    dump = (slots * nx // BLOCK + GROUPS + 1) * BLOCK
-    place = jnp.where(valid, pos.astype(I32), dump)
-    info_ref[0:nx, :] = (
-        place + (rows[0].astype(I32) + y_cells % (lanes // GROUPS) * CELLS) * CELLS
-    )
+    dump = (slots * nx // BLOCK + GROUPS) * BLOCK
+    info_ref[0:nx, :] = jnp.where(valid, pos.astype(I32), dump) + rows[0].astype(I32) * CELLS
     info_ref[nx : 2 * nx, :] = jnp.broadcast_to(
         jnp.sum(rows[2], axis=1, keepdims=True), (nx, slots)
     ).astype(I32)
@@ -271,14 +266,13 @@
 
 
 def gather_kernel(
-    nx, info, cress_hbm, high_hbm, low_hbm, part_ref, wt_hi_hbm, wt_lo_hbm,
-    cress, st_hi, st_lo, sorted_w, chosen, totals, wt_hi, wt_lo, sums, by_slot, fold, sem,
+    nx, info, meta_ref, cress_hbm, high_hbm, low_hbm, part_ref, values_ref, wt_hi_hbm, wt_lo_hbm,
+    cress, st_hi, st_lo, sorted_w, wt_hi, wt_lo, by_slot, fold, sem,
 ):
     slots = info.shape[1]
     lanes = cress.shape[2]
     tile_x = cress_hbm.shape[1]
     pieces = tile_x // lanes
-    rows = wt_hi.shape[1]
     base, count, group, blocks = block_tools(nx, lanes, info)
     loads = [
         pltpu.make_async_copy(
@@ -292,8 +286,9 @@
     ]
     for copy in loads + state_loads:
         copy.start()
-    y_line = iota((8, lanes), 0) == pieces
-    blank = jnp.where(y_line, -1.0, jnp.zeros((8, lanes), F32))
+    own_line = iota((8, lanes), 0) == pieces
+    y_lane = FEATURES + 25
+    blank = jnp.where(own_line & (iota((8, lanes), 1) == y_lane), -1.0, 0.0)
 
     def clear(b):
         where = pl.ds(pl.multiple_of(b * BLOCK, BLOCK), BLOCK)
@@ -302,24 +297,33 @@
     for g in range(GROUPS):
         pl.when(count(g) > 0)(functools.partial(clear, base(g) + count(g) - 1))
     clear(blocks)
+    part_ref[...] = jnp.zeros(part_ref.shape, F32)
+    values_ref[...] = jnp.zeros(values_ref.shape, F32)
     wide = 3 * lanes
     for g in range(GROUPS):
         fold[g] = jnp.where(
             group_of(iota((wide, lanes), 0), g) == iota((wide, lanes), 1), 1.0, 0.0
         ).astype(BF16)
+    above = jnp.zeros((FEATURES, slots), F32)
+    below = jnp.zeros((lanes - 2 * FEATURES, slots), F32)
+    for k in range(nx):
+        by_slot[k * slots : (k + 1) * slots, :] = jnp.concatenate(
+            [above, meta_ref[k], below], axis=0
+        ).T
 
     for copy in loads:
         copy.wait()
     for k in range(nx):
 
         def bring(n, carry):
+            start = pl.multiple_of(k * slots + n * STEP, STEP)
             entries = [info[k, n * STEP + m] for m in range(STEP)]
-            got = [
-                jnp.where(y_line, (lax.shift_right_logical(e, 24)).astype(F32), cress[lax.shift_right_logical(e, 12) & (CELLS - 1)])
-                for e in entries
-            ]
-            for e, row in zip(entries, got):
-                sorted_w[e & (CELLS - 1)] = row
+            for m, e in enumerate(entries):
+                sorted_w[e & (CELLS - 1)] = jnp.where(
+                    own_line,
+                    by_slot[pl.ds(start + m, 1), :],
+                    cress[lax.shift_right_logical(e, 12)],
+                )
             return carry
 
         lax.fori_loop(0, (info[nx + k, 0] + STEP - 1) // STEP, bring, 0)
@@ -329,72 +333,59 @@
     yy = (iota((BLOCK, wide), 1) % 16).astype(F32)
     lane = iota((BLOCK, lanes), 1)
 
-    def multiply(b):
-        b = jnp.minimum(b, blocks)
+    def block_sums(b):
         where = pl.ds(pl.multiple_of(b * BLOCK, BLOCK), BLOCK)
         g = group(b)
         parts = [sorted_w[where, c, :] for c in range(pieces)]
+        own = sorted_w[where, pieces, :]
         high, low = split(jnp.concatenate(parts, axis=1))
         both = dot(jnp.concatenate([high, low], axis=0), st_hi[g])
         products = both[:BLOCK] + both[BLOCK:] + dot(high, st_lo[g])
-        y_here = sorted_w[where, pieces, :]
-        y_wide = jnp.concatenate([y_here, y_here, y_here], axis=1)
-        high, low = split(jnp.where(yy == y_wide, products, 0.0))
+        y_here = own[:, y_lane : y_lane + 1]
+        y_here = y_here - jnp.floor(y_here * (1.0 / 16.0)) * 16.0
+        valid = own[:, y_lane + 1 : y_lane + 2] > 0.5
+        chosen = split(jnp.where(valid & (yy == y_here), products, 0.0))
+        both = dot(jnp.concatenate(chosen, axis=0), fold[g])
         total = jnp.sum(parts[0] + parts[1] + parts[2], axis=1, keepdims=True)
-        return where, high, low, total, [split(part.T) for part in parts]
+        result = jnp.where(lane == 24, total, both[:BLOCK] + both[BLOCK:])
+        result = jnp.where(lane < FEATURES, result, own).T
+        return b, where, result, [split(part.T) for part in parts]
+
+    per_device = part_ref.shape[2] // BLOCK
 
     def two_blocks(n, carry):
-        for m in range(2):
-            b = 2 * n - 2 + m
-            both = dot(chosen[m], fold[group(b)])
-            result = jnp.where(lane == 24, totals[m], both[:BLOCK] + both[BLOCK:])
-            start = jnp.where(b < 0, rows + m * BLOCK, b * BLOCK)
-            sums[pl.ds(pl.multiple_of(start, BLOCK), BLOCK), :] = result
-        for m, (where, high, low, total, turned) in enumerate(
-            [multiply(2 * n), multiply(2 * n + 1)]
-        ):
-            chosen[m, :BLOCK, :] = high
-            chosen[m, BLOCK:, :] = low
-            totals[m] = jnp.broadcast_to(total, (BLOCK, lanes))
+        for b, where, result, turned in [block_sums(2 * n), block_sums(2 * n + 1)]:
+            k = b // per_device
+            here = pl.ds(pl.multiple_of((b - k * per_device) * BLOCK, BLOCK), BLOCK)
+            part_ref[k, :, here] = result[:FEATURES]
+            values_ref[k, :, here] = result[FEATURES : 2 * FEATURES]
             for c in range(pieces):
                 wt_hi[c * lanes : (c + 1) * lanes, where] = turned[c][0]
                 wt_lo[c * lanes : (c + 1) * lanes, where] = turned[c][1]
         return carry
 
-    lax.fori_loop(0, (blocks + 1) // 2 + 1, two_blocks, 0)
+    lax.fori_loop(0, (blocks + 1) // 2, two_blocks, 0)
     stores = [
         pltpu.make_async_copy(wt_hi, wt_hi_hbm, sem.at[5]),
         pltpu.make_async_copy(wt_lo, wt_lo_hbm, sem.at[6]),
     ]
     for copy in stores:
         copy.start()
-
-    by_slot[...] = jnp.zeros(by_slot.shape, F32)
-    for k in range(nx):
-
-        def give(n, carry):
-            start = pl.multiple_of(k * slots + n * STEP, STEP)
-            entries = [info[k, n * STEP + m] for m in range(STEP)]
-            got = [sums[pl.ds(e & (CELLS - 1), 1), :] for e in entries]
-            for m in range(STEP):
-                by_slot[pl.ds(start + m, 1), :] = got[m]
-            return carry
-
-        lax.fori_loop(0, (info[nx + k, 0] + STEP - 1) // STEP, give, 0)
-        part_ref[k] = by_slot[k * slots : (k + 1) * slots, :].T[:FEATURES]
     for copy in stores:
         copy.wait()
 
 
 def reduce_kernel(
-    nx, part_ref, at_ref, vert_ref, xh_ref, yh_ref, state_hbm, out_ref, base_hbm,
-    plane, moved, rs, ag, load_sem, store_sem, send1, recv1, send2, recv2,
+    nx, part_ref, vert_ref, xh_ref, yh_ref, values_hbm, state_hbm, out_ref, base_hbm,
+    plane, moved, rs, ag, values, load_sem, own_sem, store_sem, send1, recv1, send2, recv2,
 ):
     i, j = lax.axis_index("gx"), lax.axis_index("gy")
     planes, padded_x, lanes = plane.shape
     tile_x = padded_x - 16
     load = pltpu.make_async_copy(state_hbm, plane.at[:, 8 : 8 + tile_x, :], load_sem)
     load.start()
+    own = pltpu.make_async_copy(values_hbm.at[i], values, own_sem)
+    own.start()
     barrier = pltpu.get_barrier_semaphore()
     for d in range(1, nx):
         pl.semaphore_signal(
@@ -449,7 +440,8 @@
     vert = jnp.concatenate([vert_ref[...], jnp.zeros((8, lanes), F32)], axis=0)
     same = iota((FEATURES, FEATURES), 0) // 8 == iota((FEATURES, FEATURES), 1) // 8
     gram = jnp.where(same, dot_t(vert, vert, HIGHEST), 0.0)
-    at = at_ref[...]
+    own.wait()
+    at = values[...]
     row = iota(at.shape, 0)
 
     pl.semaphore_wait(barrier, nx - 1)
@@ -500,10 +492,9 @@
 
 
 def update_kernel(
-    nx, info, spread_ref, meta_ref, wt_hi_hbm, wt_lo_hbm, base_hbm,
-    out_hbm, moved, wt_hi, wt_lo, by_slot, sorted_s, right, num, weights, widen, sem,
+    nx, info, spread_ref, values_ref, wt_hi_hbm, wt_lo_hbm, base_hbm,
+    out_hbm, moved, wt_hi, wt_lo, right, num, weights, widen, sem,
 ):
-    slots = spread_ref.shape[2]
     planes, tile_x, lanes = moved.shape
     base, count, group, blocks = block_tools(nx, lanes, info)
     load_h = pltpu.make_async_copy(wt_hi_hbm, wt_hi, sem.at[1])
@@ -513,13 +504,6 @@
     load_l.start()
     load_s.start()
 
-    def clear(b):
-        where = pl.ds(pl.multiple_of(b * BLOCK, BLOCK), BLOCK)
-        sorted_s[where, :] = jnp.full((BLOCK, lanes), -1.0, F32)
-
-    for g in range(GROUPS):
-        pl.when(count(g) > 0)(functools.partial(clear, base(g) + count(g) - 1))
-    clear(blocks)
     wide = 3 * lanes
     for g in range(GROUPS):
         widen[g] = jnp.where(
@@ -528,31 +512,21 @@
     num[...] = jnp.zeros(num.shape, F32)
     weights[...] = jnp.zeros(weights.shape, F32)
 
-    pad = jnp.zeros((lanes - FEATURES, slots), F32)
-    for k in range(nx):
-        by_slot[k * slots : (k + 1) * slots, :] = jnp.concatenate(
-            [spread_ref[k], meta_ref[k], pad], axis=0
-        ).T
-
-        def bring(n, carry):
-            start = pl.multiple_of(k * slots + n * STEP, STEP)
-            entries = [info[k, n * STEP + m] for m in range(STEP)]
-            got = [by_slot[pl.ds(start + m, 1), :] for m in range(STEP)]
-            for e, row in zip(entries, got):
-                sorted_s[pl.ds(e & (CELLS - 1), 1), :] = row
-            return carry
-
-        lax.fori_loop(0, (info[nx + k, 0] + STEP - 1) // STEP, bring, 0)
-
     yy = iota((BLOCK, wide), 1) % 16
     load_h.wait()
     load_l.wait()
 
     right[...] = jnp.zeros(right.shape, BF16)
+    per_device = spread_ref.shape[2] // BLOCK
+    pad = jnp.zeros((lanes - FEATURES, BLOCK), F32)
 
     def widened(b):
-        where = pl.ds(pl.multiple_of(jnp.minimum(b, blocks) * BLOCK, BLOCK), BLOCK)
-        value = sorted_s[where, :]
+        b = jnp.minimum(b, blocks)
+        k = b // per_device
+        here = pl.ds(pl.multiple_of((b - k * per_device) * BLOCK, BLOCK), BLOCK)
+        value = jnp.concatenate(
+            [spread_ref[k, :, here], values_ref[k, planes:, here], pad], axis=0
+        ).T
         y_here = value[:, 25:26].astype(I32)
         match = (value[:, 26:27] > 0.5) & (yy == y_here % 16)
         both = dot(jnp.concatenate(split(value), axis=0), widen[group(b)])
@@ -633,11 +607,8 @@
         pltpu.VMEM(grouped, BF16),
         pltpu.VMEM(grouped, BF16),
         pltpu.VMEM((rows + 8, 8, lanes), F32),
-        pltpu.VMEM((2, 2 * BLOCK, 3 * lanes), BF16),
-        pltpu.VMEM((2, BLOCK, lanes), F32),
         pltpu.VMEM((tile_x, rows), BF16),
         pltpu.VMEM((tile_x, rows), BF16),
-        pltpu.VMEM((rows + 2 * BLOCK, lanes), F32),
         pltpu.VMEM((nx * slots, lanes), F32),
         pltpu.VMEM((GROUPS, 3 * lanes, lanes), BF16),
         pltpu.SemaphoreType.DMA((7,)),
@@ -650,8 +621,6 @@
         pltpu.VMEM((planes, tile_x, lanes), F32),
         pltpu.VMEM((tile_x, rows), BF16),
         pltpu.VMEM((tile_x, rows), BF16),
-        pltpu.VMEM((nx * slots, lanes), F32),
-        pltpu.VMEM((rows + 8, lanes), F32),
         pltpu.VMEM((2, 3 * BLOCK, 4 * lanes), BF16),
         pltpu.VMEM(grouped, F32),
         pltpu.VMEM((GROUPS, tile_x, lanes), F32),
@@ -666,7 +635,8 @@
     recs = obs_val.shape[0]
     cap = max(2, 2 * recs // ny)
     slots = ny * cap
-    rows = (slots * nx // BLOCK + GROUPS + 1) * BLOCK
+    rows = (slots * nx // BLOCK + GROUPS) * BLOCK
+    chunk = rows // nx
     state = model_state.reshape(planes, tile_x, lanes)
     vert = vertical.reshape(planes, vertical.shape[2])
     shape = jax.ShapeDtypeStruct
@@ -674,26 +644,25 @@
     limit = 56 * 1024 * 1024
 
     grouped = (GROUPS, tile_x, fields * lanes)
-    at, info, meta, xh, yh, st_hi, st_lo = pl.pallas_call(
+    info, meta, xh, yh, st_hi, st_lo = pl.pallas_call(
         functools.partial(dispatch_kernel, nx, ny),
         out_shape=(
-            shape((FEATURES, slots), F32),
             shape((2 * nx + GROUPS, slots), I32),
-            shape((nx, 8, slots), F32),
+            shape((nx, FEATURES, slots), F32),
             shape((2, planes, lanes), F32),
             shape((2 * planes, tile_x), F32),
             shape(grouped, BF16),
             shape(grouped, BF16),
         ),
         in_specs=[vmem()] * 5 + [hbm()],
-        out_specs=[vmem()] * 5 + [hbm()] * 2,
+        out_specs=[vmem()] * 4 + [hbm()] * 2,
         scratch_shapes=[
             pltpu.VMEM((planes, tile_x, lanes), F32),
             pltpu.VMEM(grouped, BF16),
             pltpu.VMEM(grouped, BF16),
             pltpu.VMEM((slots, lanes), F32),
             pltpu.VMEM((slots, lanes), F32),
-            pltpu.VMEM((nx, 8, slots), F32),
+            pltpu.VMEM((nx, FEATURES, slots), F32),
             pltpu.VMEM((3, nx, slots), F32),
             pltpu.VMEM((2, planes, lanes), F32),
             pltpu.VMEM((2 * planes, tile_x), F32),
@@ -717,30 +686,33 @@
         vert, state,
     )
 
-    part, wt_hi, wt_lo = pl.pallas_call(
+    part, values, wt_hi, wt_lo = pl.pallas_call(
         functools.partial(gather_kernel, nx),
         out_shape=(
-            shape((nx, FEATURES, slots), F32),
+            shape((nx, FEATURES, chunk), F32),
+            shape((nx, FEATURES, chunk), F32),
             shape((tile_x, rows), BF16),
             shape((tile_x, rows), BF16),
         ),
-        in_specs=[smem()] + [hbm()] * 3,
-        out_specs=[vmem()] + [hbm()] * 2,
+        in_specs=[smem(), vmem()] + [hbm()] * 3,
+        out_specs=[vmem()] * 2 + [hbm()] * 2,
         scratch_shapes=gather_scratch(nx, slots, rows, cressman.shape, grouped, lanes),
         compiler_params=pltpu.CompilerParams(vmem_limit_bytes=limit),
         name="column_sums",
-    )(info, cressman, st_hi, st_lo)
+    )(info, meta, cressman, st_hi, st_lo)
 
     spread, base = pl.pallas_call(
         functools.partial(reduce_kernel, nx),
-        out_shape=(shape((nx, planes, slots), F32), shape((planes, tile_x, lanes), F32)),
-        in_specs=[vmem()] * 5 + [hbm()],
+        out_shape=(shape((nx, planes, chunk), F32), shape((planes, tile_x, lanes), F32)),
+        in_specs=[vmem()] * 4 + [hbm()] * 2,
         out_specs=[vmem(), hbm()],
         scratch_shapes=[
             pltpu.VMEM((planes, tile_x + 16, lanes), F32),
             pltpu.VMEM((planes, tile_x, lanes), F32),
-            pltpu.VMEM((nx, FEATURES, slots), F32),
-            pltpu.VMEM((nx, planes, slots), F32),
+            pltpu.VMEM((nx, FEATURES, chunk), F32),
+            pltpu.VMEM((nx, planes, chunk), F32),
+            pltpu.VMEM((FEATURES, chunk), F32),
+            dma,
             dma,
             dma((2,)),
             dma((nx,)),
@@ -752,7 +724,7 @@
             collective_id=1, has_side_effects=True, vmem_limit_bytes=limit
         ),
         name="innovations",
-    )(part, at, vert, xh, yh, state)
+    )(part, vert, xh, yh, values, state)
 
     out = pl.pallas_call(
         functools.partial(update_kernel, nx),
@@ -762,7 +734,7 @@
         scratch_shapes=update_scratch(nx, slots, rows, grouped, planes, lanes),
         compiler_params=pltpu.CompilerParams(vmem_limit_bytes=limit),
         name="update",
-    )(info, spread, meta, wt_hi, wt_lo, base)
+    )(info, spread, values, wt_hi, wt_lo, base)
     return out.reshape(model_state.shape)
 
 

time: 81.7 us -> 79.6 us (0.974)
  the two profiles are of different devices: /device:TPU:35 before, /device:TPU:5 now
where the time goes in v4:
time: 79.6 us; the launch traced here: 79.1 us
  Pallas kernels  79.1 us (99%)
    pallas_call x1, Pallas kernels, local(): pl.pallas_call(functools.partial(gather_kernel, nx), out_shape=(shape((nx...  26.1 us
    pallas_call x1, Pallas kernels, local(): pl.pallas_call(functools.partial(dispatch_kernel, nx, ny), out_shape=(sha...  19.7 us
    pallas_call x1, Pallas kernels, local(): pl.pallas_call(functools.partial(reduce_kernel, nx), out_shape=(shape((nx...  16.8 us
    pallas_call x1, Pallas kernels, local(): pl.pallas_call(functools.partial(update_kernel, nx), out_shape=shape((pla...  16.5 us

profile of v4, /device:TPU:5, one launch (start us, length us, event | category | flops | bytes accessed | tf_op | source)
XLA Modules:
  0.0 79.1 jit_solution(1294343554246499051)
XLA Ops:
  0.0 19.7 %dispatch.1 = (s32[24,256]{1,0:T(8,128)}, f32[8,32,256]{2,1,0:T(8,128)}, f32[2,24,128]{2,1,0:T(8,128)}, f32[48,384]{1,0:T(8,128)}, bf16[8,384,384]{2,1,0:T(8,128)(2,1)}, /*index=5*/bf16[8,384,384]{2,1,0:T(8,128)(2,1)}) custom-call(f32[128,384]{1,0:T(8,128)} %obs_ref.1, s32[1,128]{1,0:T(1,128)} %bitcast.10, s32[1,128]{1,0:T(1,128)} %bitcast.11, ...), custom_call_target="tpu_custom_call" | custom-call | tf_op jit(solution)/shard_map/dispatch/pallas_call | solution.py:647
  19.7 26.1 %column_sums.1 = (f32[8,32,384]{2,1,0:T(8,128)}, f32[8,32,384]{2,1,0:T(8,128)}, bf16[384,3072]{1,0:T(8,128)(2,1)}, bf16[384,3072]{1,0:T(8,128)(2,1)}) custom-call(s32[24,256]{1,0:T(8,128)} %get-tuple-element.17.info, f32[8,32,256]{2,1,0:T(8,128)} %get-tuple-element.18.meta_ref, f32[3072,384]{1,0:T(8,128)} %cress_hbm.1, ...), custom_call_target="tpu_custom_call" | custom-call | tf_op jit(solution)/shard_map/column_sums/pallas_call | solution.py:689
  45.8 16.8 %innovations.1 = (f32[8,24,384]{2,1,0:T(8,128)}, f32[24,384,128]{2,1,0:T(8,128)}) custom-call(f32[8,32,384]{2,1,0:T(8,128)} %get-tuple-element.21.part_ref, f32[24,128]{1,0:T(8,128)} %bitcast.9, f32[2,24,128]{2,1,0:T(8,128)} %get-tuple-element.22.xh_ref, f32[48,384]{1,0:T(8,128)} %get-tuple-element.23.yh_ref, ...), custom_call_target="tpu_custom_call" | custom-call | tf_op jit(solution)/shard_map/innovations/pallas_call | solution.py:704
  62.7 16.5 %update.1 = f32[24,384,128]{2,1,0:T(8,128)} custom-call(s32[24,256]{1,0:T(8,128)} %get-tuple-element.17.info, f32[8,24,384]{2,1,0:T(8,128)} %get-tuple-element.25.spread_ref, f32[8,32,384]{2,1,0:T(8,128)} %get-tuple-element.24.values_hbm.values_ref, bf16[384,3072]{1,0:T(8,128)(2,1)} %get-tuple-element.26.wt_hi_hbm, ...), custom_call_target="tpu_custom_call" | custom-call | tf_op jit(solution)/shard_map/update/pallas_call | solution.py:729

commit v5 on v4

--- a/solution.py
+++ b/solution.py
@@ -306,9 +306,12 @@
         ).astype(BF16)
     above = jnp.zeros((FEATURES, slots), F32)
     below = jnp.zeros((lanes - 2 * FEATURES, slots), F32)
+    y_row = iota((FEATURES, slots), 0) == 25
     for k in range(nx):
+        own = meta_ref[k]
+        cell = own - jnp.floor(own * (1.0 / 16.0)) * 16.0
         by_slot[k * slots : (k + 1) * slots, :] = jnp.concatenate(
-            [above, meta_ref[k], below], axis=0
+            [above, jnp.where(y_row, cell, own), below], axis=0
         ).T
 
     for copy in loads:
@@ -339,12 +342,11 @@
         parts = [sorted_w[where, c, :] for c in range(pieces)]
         own = sorted_w[where, pieces, :]
         high, low = split(jnp.concatenate(parts, axis=1))
-        both = dot(jnp.concatenate([high, low], axis=0), st_hi[g])
-        products = both[:BLOCK] + both[BLOCK:] + dot(high, st_lo[g])
-        y_here = own[:, y_lane : y_lane + 1]
-        y_here = y_here - jnp.floor(y_here * (1.0 / 16.0)) * 16.0
-        valid = own[:, y_lane + 1 : y_lane + 2] > 0.5
-        chosen = split(jnp.where(valid & (yy == y_here), products, 0.0))
+        s_hi, s_lo = st_hi[g], st_lo[g]
+        products = dot(
+            jnp.concatenate([high, low, high], axis=1), jnp.concatenate([s_hi, s_hi, s_lo], axis=0)
+        )
+        chosen = split(jnp.where(yy == own[:, y_lane : y_lane + 1], products, 0.0))
         both = dot(jnp.concatenate(chosen, axis=0), fold[g])
         total = jnp.sum(parts[0] + parts[1] + parts[2], axis=1, keepdims=True)
         result = jnp.where(lane == 24, total, both[:BLOCK] + both[BLOCK:])
@@ -353,8 +355,10 @@
 
     per_device = part_ref.shape[2] // BLOCK
 
-    def two_blocks(n, carry):
-        for b, where, result, turned in [block_sums(2 * n), block_sums(2 * n + 1)]:
+    def four_blocks(n, carry):
+        for b, where, result, turned in [
+            block_sums(jnp.minimum(4 * n + m, blocks)) for m in range(4)
+        ]:
             k = b // per_device
             here = pl.ds(pl.multiple_of((b - k * per_device) * BLOCK, BLOCK), BLOCK)
             part_ref[k, :, here] = result[:FEATURES]
@@ -364,7 +368,7 @@
                 wt_lo[c * lanes : (c + 1) * lanes, where] = turned[c][1]
         return carry
 
-    lax.fori_loop(0, (blocks + 1) // 2, two_blocks, 0)
+    lax.fori_loop(0, (blocks + 3) // 4, four_blocks, 0)
     stores = [
         pltpu.make_async_copy(wt_hi, wt_hi_hbm, sem.at[5]),
         pltpu.make_async_copy(wt_lo, wt_lo_hbm, sem.at[6]),
@@ -512,7 +516,7 @@
     num[...] = jnp.zeros(num.shape, F32)
     weights[...] = jnp.zeros(weights.shape, F32)
 
-    yy = iota((BLOCK, wide), 1) % 16
+    yy = (iota((BLOCK, wide), 1) % 16).astype(F32)
     load_h.wait()
     load_l.wait()
 
@@ -527,8 +531,7 @@
         value = jnp.concatenate(
             [spread_ref[k, :, here], values_ref[k, planes:, here], pad], axis=0
         ).T
-        y_here = value[:, 25:26].astype(I32)
-        match = (value[:, 26:27] > 0.5) & (yy == y_here % 16)
+        match = yy == value[:, 25:26]
         both = dot(jnp.concatenate(split(value), axis=0), widen[group(b)])
         s_hi = jnp.where(match, both[:BLOCK], 0.0).astype(BF16)
         s_lo = jnp.where(match, both[BLOCK:], 0.0).astype(BF16)
@@ -556,7 +559,7 @@
     lax.fori_loop(0, (blocks + 1) // 2 + 1, two_blocks, 0)
 
     load_s.wait()
-    chunk, parts = 8, 4
+    chunk, parts = 32, 4
     length = tile_x // parts
     stores = []
     for part in range(parts):

time: 79.6 us -> 74.2 us (0.932)
  the two profiles are of different devices: /device:TPU:5 before, /device:TPU:97 now
where the time goes in v5:
time: 74.2 us; the launch traced here: 74 us
  Pallas kernels  74 us (100%)
    pallas_call x1, Pallas kernels, local(): pl.pallas_call(functools.partial(gather_kernel, nx), out_shape=(shape((nx...  24.6 us
    pallas_call x1, Pallas kernels, local(): pl.pallas_call(functools.partial(dispatch_kernel, nx, ny), out_shape=(sha...  18.2 us
    pallas_call x1, Pallas kernels, local(): pl.pallas_call(functools.partial(reduce_kernel, nx), out_shape=(shape((nx...  16.8 us
    pallas_call x1, Pallas kernels, local(): pl.pallas_call(functools.partial(update_kernel, nx), out_shape=shape((pla...  14.3 us

profile of v5, /device:TPU:97, one launch (start us, length us, event | category | flops | bytes accessed | tf_op | source)
XLA Modules:
  0.0 74.0 jit_solution(8758826379998218995)
XLA Ops:
  0.0 18.2 %dispatch.1 = (s32[24,256]{1,0:T(8,128)}, f32[8,32,256]{2,1,0:T(8,128)}, f32[2,24,128]{2,1,0:T(8,128)}, f32[48,384]{1,0:T(8,128)}, bf16[8,384,384]{2,1,0:T(8,128)(2,1)}, /*index=5*/bf16[8,384,384]{2,1,0:T(8,128)(2,1)}) custom-call(f32[128,384]{1,0:T(8,128)} %obs_ref.1, s32[1,128]{1,0:T(1,128)} %bitcast.10, s32[1,128]{1,0:T(1,128)} %bitcast.11, ...), custom_call_target="tpu_custom_call" | custom-call | tf_op jit(solution)/shard_map/dispatch/pallas_call | solution.py:650
  18.2 24.6 %column_sums.1 = (f32[8,32,384]{2,1,0:T(8,128)}, f32[8,32,384]{2,1,0:T(8,128)}, bf16[384,3072]{1,0:T(8,128)(2,1)}, bf16[384,3072]{1,0:T(8,128)(2,1)}) custom-call(s32[24,256]{1,0:T(8,128)} %get-tuple-element.17.info, f32[8,32,256]{2,1,0:T(8,128)} %get-tuple-element.18.meta_ref, f32[3072,384]{1,0:T(8,128)} %cress_hbm.1, ...), custom_call_target="tpu_custom_call" | custom-call | tf_op jit(solution)/shard_map/column_sums/pallas_call | solution.py:692
  42.8 16.8 %innovations.1 = (f32[8,24,384]{2,1,0:T(8,128)}, f32[24,384,128]{2,1,0:T(8,128)}) custom-call(f32[8,32,384]{2,1,0:T(8,128)} %get-tuple-element.21.part_ref, f32[24,128]{1,0:T(8,128)} %bitcast.9, f32[2,24,128]{2,1,0:T(8,128)} %get-tuple-element.22.xh_ref, f32[48,384]{1,0:T(8,128)} %get-tuple-element.23.yh_ref, ...), custom_call_target="tpu_custom_call" | custom-call | tf_op jit(solution)/shard_map/innovations/pallas_call | solution.py:707
  59.7 14.3 %update.1 = f32[24,384,128]{2,1,0:T(8,128)} custom-call(s32[24,256]{1,0:T(8,128)} %get-tuple-element.17.info, f32[8,24,384]{2,1,0:T(8,128)} %get-tuple-element.25.spread_ref, f32[8,32,384]{2,1,0:T(8,128)} %get-tuple-element.24.values_hbm.values_ref, bf16[384,3072]{1,0:T(8,128)(2,1)} %get-tuple-element.26.wt_hi_hbm, ...), custom_call_target="tpu_custom_call" | custom-call | tf_op jit(solution)/shard_map/update/pallas_call | solution.py:732

commit v6 on v5

--- a/solution.py
+++ b/solution.py
@@ -351,9 +351,19 @@
         total = jnp.sum(parts[0] + parts[1] + parts[2], axis=1, keepdims=True)
         result = jnp.where(lane == 24, total, both[:BLOCK] + both[BLOCK:])
         result = jnp.where(lane < FEATURES, result, own).T
-        return b, where, result, [split(part.T) for part in parts]
+        return b, where, result, [
+            (high[:, c * lanes : (c + 1) * lanes].T, low[:, c * lanes : (c + 1) * lanes].T)
+            for c in range(pieces)
+        ]
 
     per_device = part_ref.shape[2] // BLOCK
+
+    def stores(n):
+        here = pl.ds(pl.multiple_of(n * 4 * BLOCK, 4 * BLOCK), 4 * BLOCK)
+        return [
+            pltpu.make_async_copy(wt_hi.at[:, here], wt_hi_hbm.at[:, here], sem.at[5 + 2 * n]),
+            pltpu.make_async_copy(wt_lo.at[:, here], wt_lo_hbm.at[:, here], sem.at[6 + 2 * n]),
+        ]
 
     def four_blocks(n, carry):
         for b, where, result, turned in [
@@ -366,17 +376,19 @@
             for c in range(pieces):
                 wt_hi[c * lanes : (c + 1) * lanes, where] = turned[c][0]
                 wt_lo[c * lanes : (c + 1) * lanes, where] = turned[c][1]
+        for copy in stores(n):
+            copy.start()
         return carry
 
-    lax.fori_loop(0, (blocks + 3) // 4, four_blocks, 0)
-    stores = [
-        pltpu.make_async_copy(wt_hi, wt_hi_hbm, sem.at[5]),
-        pltpu.make_async_copy(wt_lo, wt_lo_hbm, sem.at[6]),
-    ]
-    for copy in stores:
-        copy.start()
-    for copy in stores:
-        copy.wait()
+    steps = jnp.maximum((blocks + 3) // 4, 1)
+    lax.fori_loop(0, steps, four_blocks, 0)
+
+    def done(n, carry):
+        for copy in stores(n):
+            copy.wait()
+        return carry
+
+    lax.fori_loop(0, steps, done, 0)
 
 
 def reduce_kernel(
@@ -559,7 +571,7 @@
     lax.fori_loop(0, (blocks + 1) // 2 + 1, two_blocks, 0)
 
     load_s.wait()
-    chunk, parts = 32, 4
+    chunk, parts = 96, 4
     length = tile_x // parts
     stores = []
     for part in range(parts):
@@ -614,7 +626,7 @@
         pltpu.VMEM((tile_x, rows), BF16),
         pltpu.VMEM((nx * slots, lanes), F32),
         pltpu.VMEM((GROUPS, 3 * lanes, lanes), BF16),
-        pltpu.SemaphoreType.DMA((7,)),
+        pltpu.SemaphoreType.DMA((5 + 2 * (rows // (4 * BLOCK)),)),
     ]
 
 

time: 74.2 us -> 71.8 us (0.968)
  the two profiles are of different devices: /device:TPU:97 before, /device:TPU:67 now
where the time goes in v6:
time: 71.8 us; the launch traced here: 71.6 us
  Pallas kernels  71.6 us (100%)
    pallas_call x1, Pallas kernels, local(): pl.pallas_call(functools.partial(gather_kernel, nx), out_shape=(shape((nx...  23.2 us
    pallas_call x1, Pallas kernels, local(): pl.pallas_call(functools.partial(dispatch_kernel, nx, ny), out_shape=(sha...  17.8 us
    pallas_call x1, Pallas kernels, local(): pl.pallas_call(functools.partial(reduce_kernel, nx), out_shape=(shape((nx...  16.8 us
    pallas_call x1, Pallas kernels, local(): pl.pallas_call(functools.partial(update_kernel, nx), out_shape=shape((pla...  13.8 us

profile of v6, /device:TPU:67, one launch (start us, length us, event | category | flops | bytes accessed | tf_op | source)
XLA Modules:
  0.0 71.6 jit_solution(8372521682455535179)
XLA Ops:
  0.0 17.8 %dispatch.1 = (s32[24,256]{1,0:T(8,128)}, f32[8,32,256]{2,1,0:T(8,128)}, f32[2,24,128]{2,1,0:T(8,128)}, f32[48,384]{1,0:T(8,128)}, bf16[8,384,384]{2,1,0:T(8,128)(2,1)}, /*index=5*/bf16[8,384,384]{2,1,0:T(8,128)(2,1)}) custom-call(f32[128,384]{1,0:T(8,128)} %obs_ref.1, s32[1,128]{1,0:T(1,128)} %bitcast.10, s32[1,128]{1,0:T(1,128)} %bitcast.11, ...), custom_call_target="tpu_custom_call" | custom-call | tf_op jit(solution)/shard_map/dispatch/pallas_call | solution.py:662
  17.8 23.2 %column_sums.1 = (f32[8,32,384]{2,1,0:T(8,128)}, f32[8,32,384]{2,1,0:T(8,128)}, bf16[384,3072]{1,0:T(8,128)(2,1)}, bf16[384,3072]{1,0:T(8,128)(2,1)}) custom-call(s32[24,256]{1,0:T(8,128)} %get-tuple-element.17.info, f32[8,32,256]{2,1,0:T(8,128)} %get-tuple-element.18.meta_ref, f32[3072,384]{1,0:T(8,128)} %cress_hbm.1, ...), custom_call_target="tpu_custom_call" | custom-call | tf_op jit(solution)/shard_map/column_sums/pallas_call | solution.py:704
  41.0 16.8 %innovations.1 = (f32[8,24,384]{2,1,0:T(8,128)}, f32[24,384,128]{2,1,0:T(8,128)}) custom-call(f32[8,32,384]{2,1,0:T(8,128)} %get-tuple-element.21.part_ref, f32[24,128]{1,0:T(8,128)} %bitcast.9, f32[2,24,128]{2,1,0:T(8,128)} %get-tuple-element.22.xh_ref, f32[48,384]{1,0:T(8,128)} %get-tuple-element.23.yh_ref, ...), custom_call_target="tpu_custom_call" | custom-call | tf_op jit(solution)/shard_map/innovations/pallas_call | solution.py:719
  57.9 13.8 %update.1 = f32[24,384,128]{2,1,0:T(8,128)} custom-call(s32[24,256]{1,0:T(8,128)} %get-tuple-element.17.info, f32[8,24,384]{2,1,0:T(8,128)} %get-tuple-element.25.spread_ref, f32[8,32,384]{2,1,0:T(8,128)} %get-tuple-element.24.values_hbm.values_ref, bf16[384,3072]{1,0:T(8,128)(2,1)} %get-tuple-element.26.wt_hi_hbm, ...), custom_call_target="tpu_custom_call" | custom-call | tf_op jit(solution)/shard_map/update/pallas_call | solution.py:744

commit v7 on v6

--- a/solution.py
+++ b/solution.py
@@ -177,7 +177,7 @@
         )
         copy.start()
         second.append(copy)
-    chunk = 32
+    chunk = 96
 
     def group_chunk(n, carry):
         here = pl.ds(pl.multiple_of(n * chunk, chunk), chunk)

time: 71.8 us -> 73.3 us (1.021)
  the two profiles are of different devices: /device:TPU:67 before, /device:TPU:5 now
where the time goes in v7:
time: 73.3 us; the launch traced here: 72.8 us
  Pallas kernels  72.8 us (99%)
    pallas_call x1, Pallas kernels, local(): pl.pallas_call(functools.partial(gather_kernel, nx), out_shape=(shape((nx...  23.2 us
    pallas_call x1, Pallas kernels, local(): pl.pallas_call(functools.partial(dispatch_kernel, nx, ny), out_shape=(sha...  19.7 us
    pallas_call x1, Pallas kernels, local(): pl.pallas_call(functools.partial(reduce_kernel, nx), out_shape=(shape((nx...  16.8 us
    pallas_call x1, Pallas kernels, local(): pl.pallas_call(functools.partial(update_kernel, nx), out_shape=shape((pla...  13.1 us

profile of v7, /device:TPU:5, one launch (start us, length us, event | category | flops | bytes accessed | tf_op | source)
XLA Modules:
  0.0 72.8 jit_solution(15800546697428055567)
XLA Ops:
  0.0 19.7 %dispatch.1 = (s32[24,256]{1,0:T(8,128)}, f32[8,32,256]{2,1,0:T(8,128)}, f32[2,24,128]{2,1,0:T(8,128)}, f32[48,384]{1,0:T(8,128)}, bf16[8,384,384]{2,1,0:T(8,128)(2,1)}, /*index=5*/bf16[8,384,384]{2,1,0:T(8,128)(2,1)}) custom-call(f32[128,384]{1,0:T(8,128)} %obs_ref.1, s32[1,128]{1,0:T(1,128)} %bitcast.10, s32[1,128]{1,0:T(1,128)} %bitcast.11, ...), custom_call_target="tpu_custom_call" | custom-call | tf_op jit(solution)/shard_map/dispatch/pallas_call | solution.py:662
  19.7 23.2 %column_sums.1 = (f32[8,32,384]{2,1,0:T(8,128)}, f32[8,32,384]{2,1,0:T(8,128)}, bf16[384,3072]{1,0:T(8,128)(2,1)}, bf16[384,3072]{1,0:T(8,128)(2,1)}) custom-call(s32[24,256]{1,0:T(8,128)} %get-tuple-element.17.info, f32[8,32,256]{2,1,0:T(8,128)} %get-tuple-element.18.meta_ref, f32[3072,384]{1,0:T(8,128)} %cress_hbm.1, ...), custom_call_target="tpu_custom_call" | custom-call | tf_op jit(solution)/shard_map/column_sums/pallas_call | solution.py:704
  42.9 16.8 %innovations.1 = (f32[8,24,384]{2,1,0:T(8,128)}, f32[24,384,128]{2,1,0:T(8,128)}) custom-call(f32[8,32,384]{2,1,0:T(8,128)} %get-tuple-element.21.part_ref, f32[24,128]{1,0:T(8,128)} %bitcast.9, f32[2,24,128]{2,1,0:T(8,128)} %get-tuple-element.22.xh_ref, f32[48,384]{1,0:T(8,128)} %get-tuple-element.23.yh_ref, ...), custom_call_target="tpu_custom_call" | custom-call | tf_op jit(solution)/shard_map/innovations/pallas_call | solution.py:719
  59.7 13.1 %update.1 = f32[24,384,128]{2,1,0:T(8,128)} custom-call(s32[24,256]{1,0:T(8,128)} %get-tuple-element.17.info, f32[8,24,384]{2,1,0:T(8,128)} %get-tuple-element.25.spread_ref, f32[8,32,384]{2,1,0:T(8,128)} %get-tuple-element.24.values_hbm.values_ref, bf16[384,3072]{1,0:T(8,128)(2,1)} %get-tuple-element.26.wt_hi_hbm, ...), custom_call_target="tpu_custom_call" | custom-call | tf_op jit(solution)/shard_map/update/pallas_call | solution.py:744
